TPU v7x, 32 devices: a whole 2x2x4 slice. The times are simulated.
32 devices in a mesh: gx: 4 (over z), gy: 4 (over x, core), gz: 2 (over y).
Axes of the slice: x: 2, y: 2, z: 4, core: 2. Of those that a mesh axis runs over, the one named last changes fastest.
Arguments:
- offsets: float32 [3, 8, 16, 8, 256], P(None, 'gx', 'gy', 'gz'), may hold values from 0 to 1
- charges: float32 [8, 16, 8, 256], P('gx', 'gy', 'gz'), may hold values from -0.6 to 0.6
- counts: int32 [8, 16, 8], P('gx', 'gy', 'gz'), may hold values from 1 to 256
- owned_cell: int32 [128], P(('gx', 'gy', 'gz')), may hold values from 0 to 127, each once
- list_sources: int32 [128, 189], P(('gx', 'gy', 'gz')), may hold values from 0 to 127
- list_ops: int32 [128, 189], P(('gx', 'gy', 'gz')), may hold values from 0 to 255
- m2m: float32 [8, 121, 121], replicated, may hold values from -0.1875 to 0.1875
- m2l: bfloat16 [121, 121, 256], replicated, may hold values from -0.0390625 to 0.0390625
- l2l: float32 [8, 121, 121], replicated, may hold values from -0.5 to 0.5
Outputs:
- potential: float32 [8, 16, 8, 256], P('gx', 'gy', 'gz')
Inputs may be any that keep to these rules, and one draw needn't show every extreme that they name: `owned_cell`: a permutation of the parent cells.
All inputs are finite; a program needn't handle non-finite values.
Results may differ from a plain program's by a relative error of at most 0.0003.
Values may be sent and summed in bfloat16 or wider, within the bound.
No kernel may reach another device: no remote copies, remote signals or barrier semaphores. Data moves between devices by JAX's collectives and lax.ppermute only.
A program may use at most 64 MiB of HBM per device.

v0:
```python
import math
import functools
import numpy as np
import jax
import jax.numpy as jnp
from jax import lax
from jax.experimental import pallas as pl
from jax.experimental.pallas import tpu as pltpu
from jax.sharding import PartitionSpec as P

SOFTENING = 0.01
DELTAS = [(dx, dy, dz) for dx in (-1, 0, 1) for dy in (-1, 0, 1) for dz in (-1, 0, 1)]


def delta_tables():
    table = np.zeros((27, 64, 128), np.float32)
    for index, delta in enumerate(DELTAS):
        for axis in range(3):
            for group in range(3):
                table[index, 8 * group + axis] = 2.0 * delta[axis]
                table[index, 32 + 8 * group + axis] = delta[axis]
        table[index, 24] = sum(d * d for d in delta)
    return table


def split3(value):
    first = value.astype(jnp.bfloat16).astype(jnp.float32)
    rest = value - first
    second = rest.astype(jnp.bfloat16).astype(jnp.float32)
    third = (rest - second).astype(jnp.bfloat16).astype(jnp.float32)
    return first, second, third


def rows_of(raw, shape):
    rows = lax.broadcasted_iota(jnp.int32, shape, 0)
    padded = jnp.concatenate([raw, jnp.zeros_like(raw)], 0)
    centred = jnp.where(rows < 3, padded - 0.5, 0.0)
    square = centred * centred
    norm = square[0:1] + square[1:2] + square[2:3]
    return rows, centred, norm


def pick(rows, low, parts, high):
    first, second, third = parts
    out = jnp.where(rows == low, first, high)
    out = jnp.where(rows == low + 1, second, out)
    return jnp.where(rows == low + 2, third, out)


def source_features(raw, shape):
    rows, centred, norm = rows_of(raw, shape)
    one, two, three = split3(centred)
    ones = jnp.where((rows >= 3) & (rows < 6), 1.0, 0.0)
    norms = pick(rows, 0, split3(norm), ones)
    zero = jnp.zeros_like(one)
    first_row = jnp.where(rows == 0, 1.0, 0.0)
    groups = [one, one, one, two, two, three, norms, zero, one, two, three, first_row]
    return jnp.concatenate(groups, 0).astype(jnp.bfloat16)


def target_features(raw, shape):
    rows, centred, norm = rows_of(raw, shape)
    one, two, three = split3(centred)
    one, two, three = -2.0 * one, -2.0 * two, -2.0 * three
    lead = jnp.where(rows < 3, 1.0, 0.0)
    norms = pick(rows, 3, split3(norm + SOFTENING), lead)
    zero = jnp.zeros_like(one)
    first_row = jnp.where(rows == 0, 1.0, 0.0)
    groups = [one, two, three, one, two, one, norms, zero]
    groups += [lead, lead, lead, first_row, one, two, three, zero]
    return jnp.concatenate(groups, 0).T.astype(jnp.bfloat16)


def near_body(cells, counts, source, table, out, base, left, total):
    cells_x, cells_y, cells_z = cells
    pad_y, pad_z = cells_y + 2, cells_z + 2
    leaves = cells_x * cells_y * cells_z
    width = source.shape[-1]
    shape = (8, width)
    padded = source.shape[0]

    def fill(leaf, carry):
        base[leaf] = source_features(source[leaf], shape)
        return carry

    lax.fori_loop(0, padded, fill, 0, unroll=4)

    def home(leaf):
        a = leaf // (cells_y * cells_z)
        b = leaf // cells_z % cells_y
        c = leaf % cells_z
        return ((a + 1) * pad_y + b + 1) * pad_z + c + 1

    def fill_left(leaf, carry):
        left[leaf] = target_features(source[home(leaf)], shape)
        return carry

    lax.fori_loop(0, leaves, fill_left, 0, unroll=2)

    def block(leaf, height):
        centre = home(leaf)
        lhs = left[leaf, 0:height]
        acc = jnp.zeros((height, 128), jnp.float32)
        for index, (dx, dy, dz) in enumerate(DELTAS):
            other = centre + (dx * pad_y + dy) * pad_z + dz
            scale = table[index, 0:32]
            fixed = table[index, 32:64]
            halves = []
            for part in range(width // 128):
                lanes = slice(128 * part, 128 * part + 128)
                halves.append(
                    jnp.concatenate(
                        [base[other, 0:64, lanes], base[other, 64:96, lanes] * scale, fixed], 0
                    )
                )
            rhs = jnp.concatenate(halves, 1)
            dist2 = jnp.dot(lhs, rhs, preferred_element_type=jnp.float32)
            inverse = lax.rsqrt(dist2)
            if dx == 0 and dy == 0 and dz == 0:
                row = lax.broadcasted_iota(jnp.int32, inverse.shape, 0)
                col = lax.broadcasted_iota(jnp.int32, inverse.shape, 1)
                inverse = jnp.where(row == col, 0.0, inverse)
            weighted = inverse * source[other, 3:4]
            for part in range(width // 128):
                acc = acc + weighted[:, 128 * part : 128 * part + 128]
        total[leaf, 0:height] = acc

    step = 64

    def leaf_step(leaf, carry):
        pieces = (counts[leaf] + step - 1) // step
        for number in range(1, width // step + 1):
            last = number == width // step
            hit = (pieces >= number) if last else (pieces == number)

            @pl.when(hit)
            def _():
                block(leaf, number * step)

        return carry

    lax.fori_loop(0, leaves, leaf_step, 0)
    ones = jnp.ones((8, 128), jnp.bfloat16)
    dims = (((1,), (1,)), ((), ()))

    def finish(leaf, carry):
        first, second, third = split3(total[leaf])
        result = jnp.zeros((8, width), jnp.float32)
        for piece in (first, second, third):
            result = result + lax.dot_general(
                ones, piece.astype(jnp.bfloat16), dims, preferred_element_type=jnp.float32
            )
        slot = lax.broadcasted_iota(jnp.int32, (1, width), 1)
        out[pl.ds(leaf, 1), :] = jnp.where(slot < counts[leaf], result[0:1], 0.0)
        return carry

    lax.fori_loop(0, leaves, finish, 0, unroll=4)


def near_field(counts, padded, cells):
    leaves = cells[0] * cells[1] * cells[2]
    total, _, width = padded.shape
    table = jnp.asarray(delta_tables(), jnp.bfloat16)
    vmem = pl.BlockSpec(memory_space=pltpu.VMEM)
    return pl.pallas_call(
        functools.partial(near_body, cells),
        out_shape=jax.ShapeDtypeStruct((leaves, width), jnp.float32),
        in_specs=[pl.BlockSpec(memory_space=pltpu.SMEM), vmem, vmem],
        out_specs=vmem,
        scratch_shapes=[
            pltpu.VMEM((total, 96, width), jnp.bfloat16),
            pltpu.VMEM((leaves, width, 128), jnp.bfloat16),
            pltpu.VMEM((leaves, width, 128), jnp.float32),
        ],
        name="near",
    )(counts, padded, table)


def translate_body(shape_info, mine, table, matrix, out, store, weights, sums, sems):
    coef, per_device, lists, ops, wide = shape_info
    rows = table.shape[0]
    span = 128 // per_device
    blocks = -(-coef // span)
    chunk = sums.shape[0] // sems.shape[0]
    copies = [
        pltpu.make_async_copy(
            matrix.at[pl.ds(chunk * index, chunk)],
            store.at[pl.ds(chunk * index, chunk)],
            sems.at[index],
        )
        for index in range(sems.shape[0])
    ]
    for copy in copies:
        copy.start()

    def iota(shape, dim):
        return lax.broadcasted_iota(jnp.int32, shape, dim)

    def mask(condition):
        return jnp.where(condition, 1.0, 0.0)

    seg = 256
    head = table[:, 0:128].astype(jnp.float32)
    owned = head[:, coef : coef + 1] + 256.0 * head[:, coef + 1 : coef + 2]
    lane = iota((rows, 128), 1)
    chosen = mask((owned.astype(jnp.int32) == lane + mine[0]) & (lane < per_device))
    chosen = chosen.T[0:8].astype(jnp.bfloat16)
    entries = jnp.dot(chosen, table[:, 128 : 128 + wide * seg], preferred_element_type=jnp.float32)
    sources = entries[:, seg : 2 * seg]
    if wide == 3:
        sources = sources + 256.0 * entries[:, 2 * seg : 3 * seg]
    sources = sources.astype(jnp.int32)
    classes = entries[:, 0:seg].astype(jnp.int32)
    counted = []
    for row in range(per_device):
        from_cell = mask(iota((rows, seg), 0) == sources[row : row + 1])
        to_class = mask(
            (iota((ops, seg), 0) == classes[row : row + 1]) & (iota((ops, seg), 1) < lists)
        )
        counted.append(
            lax.dot_general(
                to_class.astype(jnp.bfloat16),
                from_cell.astype(jnp.bfloat16),
                (((1,), (1,)), ((), ())),
                preferred_element_type=jnp.float32,
            ).astype(jnp.bfloat16)
        )
    counted = jnp.concatenate(counted, 1)
    parents = table[:, 0:128]
    lane = iota((rows, 128), 1)
    for block in range(blocks):
        pick_row = iota((128, 128), 0)
        pick_col = iota((128, 128), 1)
        spread = mask((pick_row == span * block + pick_col % span) & (pick_row < coef))
        tiled = jnp.dot(parents, spread.astype(jnp.bfloat16), preferred_element_type=jnp.float32)
        stacked = jnp.concatenate(
            [jnp.where(lane // span == row, tiled, 0.0) for row in range(per_device)], 0
        )
        weights[block] = jnp.dot(
            counted, stacked.astype(jnp.bfloat16), preferred_element_type=jnp.float32
        ).astype(jnp.bfloat16)
    for index, copy in enumerate(copies):
        copy.wait()
        total = jnp.zeros((chunk, 128), jnp.float32)
        for block in range(blocks):
            height = min(span, coef - span * block)
            part = store[pl.ds(chunk * index, chunk), span * block : span * block + height, :]
            if height < span:
                fill = jnp.zeros((chunk, span - height, ops), part.dtype)
                part = jnp.concatenate([part, fill], 1)
            result = jnp.dot(
                part.reshape(chunk * span, ops), weights[block], preferred_element_type=jnp.float32
            ).reshape(chunk, span, 128)
            keep = iota((chunk, span, 128), 1) == iota((chunk, span, 128), 2) % span
            total = total + jnp.sum(jnp.where(keep, result, 0.0), 1)
        sums[pl.ds(chunk * index, chunk), :] = total
    gather = mask(iota((128, 128), 0) // span == iota((128, 128), 1)).astype(jnp.bfloat16)
    local = jnp.zeros((coef, 128), jnp.float32)
    for piece in split3(sums[...]):
        local = local + jnp.dot(
            piece.astype(jnp.bfloat16), gather, preferred_element_type=jnp.float32
        )
    out[...] = local


def translate(mine, table, matrix, per_device, lists, wide):
    coef, _, ops = matrix.shape
    pieces = next(n for n in range(11, 0, -1) if coef % n == 0)
    vmem = pl.BlockSpec(memory_space=pltpu.VMEM)
    span = 128 // per_device
    return pl.pallas_call(
        functools.partial(translate_body, (coef, per_device, lists, ops, wide)),
        out_shape=jax.ShapeDtypeStruct((coef, 128), jnp.float32),
        in_specs=[pl.BlockSpec(memory_space=pltpu.SMEM), vmem, pl.BlockSpec(memory_space=pl.ANY)],
        out_specs=vmem,
        scratch_shapes=[
            pltpu.VMEM(matrix.shape, matrix.dtype),
            pltpu.VMEM((-(-coef // span), ops, 128), jnp.bfloat16),
            pltpu.VMEM((coef, 128), jnp.float32),
            pltpu.SemaphoreType.DMA((pieces,)),
        ],
        name="translate",
    )(mine, table, matrix)


ORDER = 10
MESH_AXES = ("gx", "gy", "gz")


def extended(value, sides):
    for axis, dim in sides:
        peers, length = lax.axis_size(axis), value.shape[dim]
        last = lax.slice_in_dim(value, length - 1, length, axis=dim)
        leading = lax.slice_in_dim(value, 0, 1, axis=dim)
        if peers == 2:
            upper = lax.axis_index(axis) == 1
            other = lax.ppermute(jnp.where(upper, leading, last), axis, [(0, 1), (1, 0)])
            before = jnp.where(upper, other, 0.0)
            after = jnp.where(upper, 0.0, other)
        else:
            up = [(i, i + 1) for i in range(peers - 1)]
            before = lax.ppermute(last, axis, up)
            after = lax.ppermute(leading, axis, [(j, i) for i, j in up])
        value = jnp.concatenate([before, value, after], axis=dim)
    return value


def harmonics(relative):
    coord_x, coord_y, coord_z = (relative[0], relative[1], relative[2])
    radius2 = coord_x * coord_x + coord_y * coord_y + coord_z * coord_z
    real_part = {}
    imag_part = {}
    real_part[0, 0] = jnp.ones_like(coord_x)
    imag_part[0, 0] = jnp.zeros_like(coord_x)
    for azimuth in range(1, ORDER + 1):
        factor = 1.0 if azimuth == 1 else math.sqrt((2 * azimuth - 1) / (2 * azimuth))
        prev_re = real_part[azimuth - 1, azimuth - 1]
        prev_im = imag_part[azimuth - 1, azimuth - 1]
        real_part[azimuth, azimuth] = factor * (coord_x * prev_re - coord_y * prev_im)
        imag_part[azimuth, azimuth] = factor * (coord_x * prev_im + coord_y * prev_re)
    for azimuth in range(0, ORDER + 1):
        for degree in range(azimuth + 1, ORDER + 1):
            denom = math.sqrt(degree * degree - azimuth * azimuth)
            first = (2 * degree - 1) / denom
            next_re = first * coord_z * real_part[degree - 1, azimuth]
            next_im = first * coord_z * imag_part[degree - 1, azimuth]
            if degree - 2 >= azimuth:
                second = math.sqrt((degree - 1) ** 2 - azimuth * azimuth) / denom
                next_re = next_re - second * radius2 * real_part[degree - 2, azimuth]
                next_im = next_im - second * radius2 * imag_part[degree - 2, azimuth]
            real_part[degree, azimuth] = next_re
            imag_part[degree, azimuth] = next_im
    pieces = []
    for degree in range(ORDER + 1):
        pieces.append(real_part[degree, 0])
        for azimuth in range(1, degree + 1):
            pieces.append(real_part[degree, azimuth])
            pieces.append(imag_part[degree, azimuth])
    return pieces


def children(field):
    coef, size_x, size_y, size_z = field.shape
    split = field.reshape(coef, size_x // 2, 2, size_y // 2, 2, size_z // 2, 2)
    result = []
    for octant in range(8):
        result.append(split[:, :, octant // 4, :, octant // 2 % 2, :, octant % 2])
    return result


def columns(cell, halves, peers):
    (half_x, half_y, half_z), (_, count_y, count_z) = halves, peers
    parents_y, parents_z = half_y * count_y, half_z * count_z
    cell_a = cell // (parents_y * parents_z)
    cell_b = cell // parents_z % parents_y
    cell_c = cell % parents_z
    device = (cell_a // half_x * count_y + cell_b // half_y) * count_z + cell_c // half_z
    local = (cell_a % half_x * half_y + cell_b % half_y) * half_z + cell_c % half_z
    return device * (half_x * half_y * half_z) + local


def on_device(offsets, charges, counts, owned_cell, list_sources, list_ops, m2m, m2l, l2l):
    cells = cells_x, cells_y, cells_z = charges.shape[:3]
    width = charges.shape[3]
    leaves = cells_x * cells_y * cells_z
    halves = half_x, half_y, half_z = (cells_x // 2, cells_y // 2, cells_z // 2)
    per_device = half_x * half_y * half_z
    peers = tuple(lax.axis_size(axis) for axis in MESH_AXES)
    devices = peers[0] * peers[1] * peers[2]
    total_parents = per_device * devices
    slot_ids = jnp.arange(width, dtype=jnp.int32)
    live = (slot_ids[None, None, None, :] < counts[..., None]).astype(jnp.float32)
    charge_live = charges * live
    stacked = jnp.stack([offsets[0], offsets[1], offsets[2], charge_live], 3)
    padded = extended(stacked, (("gz", 2), ("gy", 1), ("gx", 0)))
    padded = padded.reshape(-1, 4, width)

    basis = jnp.stack(harmonics(offsets - 0.5), 0)
    coef = basis.shape[0]
    leaf_multipole = jnp.sum(basis * charge_live[None], -1)
    parent = jnp.zeros((coef, half_x, half_y, half_z), jnp.float32)
    for octant, child in enumerate(children(leaf_multipole)):
        parent = parent + jnp.tensordot(
            m2m[octant], child, axes=(1, 0), precision=lax.Precision.HIGHEST
        )
    parent_rows = parent.astype(jnp.bfloat16).reshape(coef, per_device).T

    lists = list_sources.shape[1]
    wide = 2 if total_parents <= 256 else 3
    owner_columns = columns(owned_cell, halves, peers)[:, None]
    source_columns = columns(list_sources, halves, peers)

    def segment(values, size):
        values = values.astype(jnp.bfloat16)
        return jnp.pad(values, ((0, 0), (0, size - values.shape[1])))

    pieces = [
        parent_rows,
        segment(owner_columns % 256, 1),
        segment(owner_columns // 256, 127 - coef),
        segment(list_ops, 256),
        segment(source_columns % 256, 256),
    ]
    if wide == 3:
        pieces.append(segment(source_columns // 256, 256))
    payload = jnp.concatenate(pieces, 1)
    spread = jnp.broadcast_to(payload[None], (devices,) + payload.shape)
    table = lax.all_to_all(spread, MESH_AXES, 0, 0).reshape(total_parents, payload.shape[1])

    near = near_field(counts.reshape(-1), padded, cells).reshape(charges.shape)

    mine = (lax.axis_index(MESH_AXES) * per_device).astype(jnp.int32).reshape(1)
    local = translate(mine, table, m2l, per_device, lists, wide)
    parent_local = local[:, :per_device].reshape(coef, half_x, half_y, half_z)
    pieces = [
        jnp.tensordot(l2l[octant], parent_local, axes=(1, 0), precision=lax.Precision.HIGHEST)
        for octant in range(8)
    ]
    joined = jnp.stack(pieces, 0).reshape((2, 2, 2, coef, half_x, half_y, half_z))
    leaf_local = jnp.transpose(joined, (3, 4, 0, 5, 1, 6, 2)).reshape(
        coef, cells_x, cells_y, cells_z
    )
    far = jnp.sum(basis * leaf_local[..., None], 0)
    return live * (near + far)


def solution(mesh):
    placed = (
        P(None, "gx", "gy", "gz", None),
        P("gx", "gy", "gz", None),
        P("gx", "gy", "gz"),
        P(("gx", "gy", "gz")),
        P(("gx", "gy", "gz"), None),
        P(("gx", "gy", "gz"), None),
        P(),
        P(),
        P(),
    )
    return jax.shard_map(
        on_device, mesh=mesh, in_specs=placed, out_specs=P("gx", "gy", "gz", None), check_vma=False
    )
```

profile of v0, /device:TPU:18, one launch (start us, length us, event | category | flops | bytes accessed | tf_op | source)
XLA Modules:
  0.0 94.6 jit_solution(5668251530618314584)
XLA Ops:
  0.0 0.8 slice_bitcast_fusion.2
  0.8 0.8 fusion.56
  1.7 1.6 %collective-permute-start = (f32[2,4,1,4,256]{4,2,1,0,3:T(1,128)S(1)}, f32[2,4,1,4,256]{4,2,1,0,3:T(1,128)S(1)}, u32[]{:S(2)}, u32[]{:S(2)}) collective-permute-start(f32[2,4,1,4,256]{4,2,1,0,3:T(1,128)S(1)} %broadcast_select_fusion.2), channel_id=1, source_target_pairs={{0,1},{1,0},{2,3},{3,2},{4,5},{5,4},{6,7},{7,6},{8,9},{9,8},{10,11... | collective-permute-start | bytes 98312 | tf_op jit(solution)/shard_map/ppermute | solution.py:297
  3.3 0.9 broadcast_add_fusion
  4.2 0.8 fusion.11
  11.4 1.9 %copy-done = f32[121,2,4,4,256]{4,3,2,1,0:T(4,128)} copy-done((f32[121,2,4,4,256]{4,3,2,1,0:T(4,128)}, f32[121,2,4,4,256]{4,3,2,1,0:T(4,128)S(1)}, u32[]{:S(2)}) %copy-start) | copy-done | bytes 3964952
  13.2 1.5 %multiply_reduce_fusion.1 = f32[121,2,4,4]{3,2,1,0:T(4,128)S(1)} fusion(f32[121,2,4,4,256]{4,3,2,1,0:T(4,128)S(1)} %constant_dynamic-update-slice_fusion, f32[2,4,4,256]{3,2,1,0:T(4,128)S(1)} %fusion.11), kind=kLoop, calls=%fused_computation.1 | loop fusion | flops 1978592 | bytes 4013184 | tf_op jit(solution)/shard_map/reduce_sum | solution.py:380
  17.5 1.9 %collective-permute-start.1 = (f32[2,1,6,4,256]{4,2,1,0,3:T(8,128)S(1)}, f32[2,1,6,4,256]{4,2,1,0,3:T(8,128)S(1)}, u32[]{:S(2)}, u32[]{:S(2)}) collective-permute-start(f32[2,1,6,4,256]{4,2,1,0,3:T(8,128)S(1)} %get-tuple-element.63), channel_id=1, source_target_pairs={{0,2},{2,4},{4,6},{1,3},{3,5},{5,7},{8,10},{10,12},{12,14},{9,11},... | collective-permute-start | bytes 147464 | tf_op jit(solution)/shard_map/ppermute | solution.py:302
  19.4 3.6 %collective-permute-start.2 = (f32[2,1,6,4,256]{4,2,1,0,3:T(8,128)S(1)}, f32[2,1,6,4,256]{4,2,1,0,3:T(8,128)S(1)}, u32[]{:S(2)}, u32[]{:S(2)}) collective-permute-start(f32[2,1,6,4,256]{4,2,1,0,3:T(8,128)S(1)} %get-tuple-element.64), channel_id=1, source_target_pairs={{2,0},{4,2},{6,4},{3,1},{5,3},{7,5},{10,8},{12,10},{14,12},{11,9},... | collective-permute-start | bytes 147464 | tf_op jit(solution)/shard_map/ppermute | solution.py:303
  23.4 0.7 broadcast_in_dim.12
  24.2 5.0 %all-to-all-start = ((bf16[32,4,640]{2,1,0:T(4,128)(2,1)}), bf16[32,4,640]{2,1,0:T(4,128)(2,1)S(1)}, u32[]{:S(2)}, u32[]{:S(2)}) async-start(bf16[32,4,640]{2,1,0:T(4,128)(2,1)} %broadcast_in_dim.12), calls=%async_computation | async-start | bytes 327680 | tf_op jit(solution)/shard_map/all_to_all | solution.py:408
  29.1 0.6 reshape.138.counts
  29.9 3.4 %collective-permute-start.3 = (f32[1,6,6,4,256]{4,2,1,0,3:T(8,128)S(1)}, f32[1,6,6,4,256]{4,2,1,0,3:T(8,128)S(1)}, u32[]{:S(2)}, u32[]{:S(2)}) collective-permute-start(f32[1,6,6,4,256]{4,2,1,0,3:T(8,128)S(1)} %get-tuple-element.61), channel_id=1, source_target_pairs={{0,8},{8,16},{16,24},{1,9},{9,17},{17,25},{2,10},{10,18},{18,26},{... | collective-permute-start | bytes 442376 | tf_op jit(solution)/shard_map/ppermute | solution.py:302
  33.3 2.6 %collective-permute-start.4 = (f32[1,6,6,4,256]{4,2,1,0,3:T(8,128)S(1)}, f32[1,6,6,4,256]{4,2,1,0,3:T(8,128)S(1)}, u32[]{:S(2)}, u32[]{:S(2)}) collective-permute-start(f32[1,6,6,4,256]{4,2,1,0,3:T(8,128)S(1)} %get-tuple-element.62), channel_id=1, source_target_pairs={{8,0},{16,8},{24,16},{9,1},{17,9},{25,17},{10,2},{18,10},{26,18},{... | collective-permute-start | bytes 442376 | tf_op jit(solution)/shard_map/ppermute | solution.py:303
  36.3 2.4 %collective-permute-done.3 = f32[1,6,6,4,256]{4,2,1,0,3:T(8,128)S(1)} collective-permute-done((f32[1,6,6,4,256]{4,2,1,0,3:T(8,128)S(1)}, f32[1,6,6,4,256]{4,2,1,0,3:T(8,128)S(1)}, u32[]{:S(2)}, u32[]{:S(2)}) %collective-permute-start.3) | collective-permute-done | bytes 147488 | tf_op jit(solution)/shard_map/ppermute | solution.py:302
  38.7 3.2 %collective-permute-done.4 = f32[1,6,6,4,256]{4,2,1,0,3:T(8,128)S(1)} collective-permute-done((f32[1,6,6,4,256]{4,2,1,0,3:T(8,128)S(1)}, f32[1,6,6,4,256]{4,2,1,0,3:T(8,128)S(1)}, u32[]{:S(2)}, u32[]{:S(2)}) %collective-permute-start.4) | collective-permute-done | bytes 147488 | tf_op jit(solution)/shard_map/ppermute | solution.py:303
  42.0 1.2 %copy.68 = f32[4,6,6,4,256]{4,3,2,1,0:T(4,128)} copy(f32[4,6,6,4,256]{4,2,1,0,3:T(8,128)S(1)} %pad_maximum_fusion) | data formatting | bytes 1179648 | tf_op jit(solution)/shard_map/concatenate | solution.py:304
  43.2 35.9 %near.1 = f32[32,256]{1,0:T(8,128)} custom-call(s32[32]{0:T(128)} %reshape.138.counts, f32[144,4,256]{2,1,0:T(4,128)} %bitcast.178, bf16[27,64,128]{2,1,0:T(8,128)(2,1)} %constant.436.clone.table), custom_call_target="tpu_custom_call" | custom-call | tf_op jit(solution)/shard_map/near/pallas_call | solution.py:165
  79.1 0.8 reshape.140
  79.9 0.7 reshape.152.table
  80.6 7.4 %translate.1 = f32[121,128]{1,0:T(8,128)} custom-call(s32[1]{0:T(128)} %bitcast.5.mine, bf16[128,640]{1,0:T(8,128)(2,1)} %reshape.152.table, bf16[121,121,256]{2,1,0:T(8,128)(2,1)} %matrix.1), custom_call_target="tpu_custom_call" | custom-call | tf_op jit(solution)/shard_map/translate/pallas_call | solution.py:271
  88.0 0.9 copy.88
  91.1 2.8 %multiply_reduce_fusion = f32[2,4,4,256]{3,2,1,0:T(4,128)S(1)} fusion(f32[121,2,4,4,256]{4,3,2,1,0:T(4,128)} %copy-done, f32[121,2,4,4]{3,2,1,0:T(4,128)S(1)} %copy.98), kind=kLoop, calls=%fused_computation | loop fusion | flops 1974272 | bytes 4013184 | tf_op jit(solution)/shard_map/reduce_sum | solution.py:423
  93.9 0.7 add_select_fusion
  (176 shorter events, 11.9 us)
Async XLA Ops:
  1.7 15.7 %collective-permute-start = (f32[2,4,1,4,256]{4,2,1,0,3:T(1,128)S(1)}, f32[2,4,1,4,256]{4,2,1,0,3:T(1,128)S(1)}, u32[]{:S(2)}, u32[]{:S(2)}) collective-permute-start(f32[2,4,1,4,256]{4,2,1,0,3:T(1,128)S(1)} %broadcast_select_fusion.2), channel_id=1, source_target_pairs={{0,1},{1,0},{2,3},{3,2},{4,5},{5,4},{6,7},{7,6},{8,9},{9,8},{10,11... | collective-permute-start | bytes 98312 | tf_op jit(solution)/shard_map/ppermute | solution.py:297
  9.8 5.2 %copy-start.1 = (f32[8,121,121]{2,0,1:T(8,128)S(1)}, f32[8,121,121]{2,0,1:T(8,128)}, u32[]{:S(2)}) copy-start(f32[8,121,121]{2,0,1:T(8,128)} %param.16) | copy-start | bytes 1405540
  10.6 4.8 %copy-start.4 = (s32[4,189]{1,0:T(4,128)S(1)}, s32[4,189]{1,0:T(4,128)}, u32[]{:S(2)}) copy-start(s32[4,189]{1,0:T(4,128)} %param.14) | copy-start | bytes 9076
  10.9 6.4 %copy-start.6 = (s32[4]{0:T(128)S(1)}, s32[4]{0:T(128)}, u32[]{:S(2)}) copy-start(s32[4]{0:T(128)} %param.13) | copy-start | bytes 52
  11.1 12.1 %copy-start.5 = (s32[4,189]{1,0:T(4,128)S(1)}, s32[4,189]{1,0:T(4,128)}, u32[]{:S(2)}) copy-start(s32[4,189]{1,0:T(4,128)} %param.15) | copy-start | bytes 9076
  11.3 17.8 %copy-start.3 = (s32[2,4,4]{2,1,0:T(4,128)S(1)}, s32[2,4,4]{2,1,0:T(4,128)}, u32[]{:S(2)}) copy-start(s32[2,4,4]{2,1,0:T(4,128)} %param.12) | copy-start | bytes 388
  11.4 1.9 %copy-start = (f32[121,2,4,4,256]{4,3,2,1,0:T(4,128)}, f32[121,2,4,4,256]{4,3,2,1,0:T(4,128)S(1)}, u32[]{:S(2)}) copy-start(f32[121,2,4,4,256]{4,3,2,1,0:T(4,128)S(1)} %constant_dynamic-update-slice_fusion) | copy-start | bytes 11894788
  13.2 22.7 %copy-start.2 = (f32[8,121,121]{2,0,1:T(8,128)S(1)}, f32[8,121,121]{2,0,1:T(8,128)}, u32[]{:S(2)}) copy-start(f32[8,121,121]{2,0,1:T(8,128)} %param.18) | copy-start | bytes 1405540
  17.5 12.3 %collective-permute-start.1 = (f32[2,1,6,4,256]{4,2,1,0,3:T(8,128)S(1)}, f32[2,1,6,4,256]{4,2,1,0,3:T(8,128)S(1)}, u32[]{:S(2)}, u32[]{:S(2)}) collective-permute-start(f32[2,1,6,4,256]{4,2,1,0,3:T(8,128)S(1)} %get-tuple-element.63), channel_id=1, source_target_pairs={{0,2},{2,4},{4,6},{1,3},{3,5},{5,7},{8,10},{10,12},{12,14},{9,11},... | collective-permute-start | bytes 147464 | tf_op jit(solution)/shard_map/ppermute | solution.py:302
  19.4 10.3 %collective-permute-start.2 = (f32[2,1,6,4,256]{4,2,1,0,3:T(8,128)S(1)}, f32[2,1,6,4,256]{4,2,1,0,3:T(8,128)S(1)}, u32[]{:S(2)}, u32[]{:S(2)}) collective-permute-start(f32[2,1,6,4,256]{4,2,1,0,3:T(8,128)S(1)} %get-tuple-element.64), channel_id=1, source_target_pairs={{2,0},{4,2},{6,4},{3,1},{5,3},{7,5},{10,8},{12,10},{14,12},{11,9},... | collective-permute-start | bytes 147464 | tf_op jit(solution)/shard_map/ppermute | solution.py:303
  24.2 55.7 %all-to-all-start = ((bf16[32,4,640]{2,1,0:T(4,128)(2,1)}), bf16[32,4,640]{2,1,0:T(4,128)(2,1)S(1)}, u32[]{:S(2)}, u32[]{:S(2)}) async-start(bf16[32,4,640]{2,1,0:T(4,128)(2,1)} %broadcast_in_dim.12), calls=%async_computation | async-start | bytes 327680 | tf_op jit(solution)/shard_map/all_to_all | solution.py:408
  29.9 8.8 %collective-permute-start.3 = (f32[1,6,6,4,256]{4,2,1,0,3:T(8,128)S(1)}, f32[1,6,6,4,256]{4,2,1,0,3:T(8,128)S(1)}, u32[]{:S(2)}, u32[]{:S(2)}) collective-permute-start(f32[1,6,6,4,256]{4,2,1,0,3:T(8,128)S(1)} %get-tuple-element.61), channel_id=1, source_target_pairs={{0,8},{8,16},{16,24},{1,9},{9,17},{17,25},{2,10},{10,18},{18,26},{... | collective-permute-start | bytes 442376 | tf_op jit(solution)/shard_map/ppermute | solution.py:302
  33.3 8.5 %collective-permute-start.4 = (f32[1,6,6,4,256]{4,2,1,0,3:T(8,128)S(1)}, f32[1,6,6,4,256]{4,2,1,0,3:T(8,128)S(1)}, u32[]{:S(2)}, u32[]{:S(2)}) collective-permute-start(f32[1,6,6,4,256]{4,2,1,0,3:T(8,128)S(1)} %get-tuple-element.62), channel_id=1, source_target_pairs={{8,0},{16,8},{24,16},{9,1},{17,9},{25,17},{10,2},{18,10},{26,18},{... | collective-permute-start | bytes 442376 | tf_op jit(solution)/shard_map/ppermute | solution.py:303
where the time goes:
time: 95.7 us; the launch traced here: 94.6 us
  Pallas kernels  43.3 us (45%)
  starting transfers between devices  18.1 us (19%)
  other arithmetic  14.2 us (15%)
  local copies, waits for them, and re-layouts  9.26 us (10%)
  waiting for transfers between devices  5.6 us (6%)
  matrix products  3.68 us (4%)
    pallas_call x1, Pallas kernels, near_field(): pl.pallas_call(functools.partial(near_body, cells), out_shape=jax.ShapeDt...  35.9 us
    pallas_call x1, Pallas kernels, translate(): pl.pallas_call(functools.partial(translate_body, (coef, per_device, lists...  7.38 us
    ppermute x2, starting transfers between devices, extended(): after = lax.ppermute(leading, axis, [(j, i) for i, j in up])  6.23 us
    unnamed x118, other arithmetic  6.04 us
    ppermute x2, starting transfers between devices, extended(): before = lax.ppermute(last, axis, up)  5.35 us
    all_to_all x1, starting transfers between devices, on_device(): lax.all_to_all(spread, MESH_AXES, 0, 0)  4.95 us
    ppermute x2, waiting for transfers between devices, extended(): after = lax.ppermute(leading, axis, [(j, i) for i, j in up])  3.17 us
    reduce_sum x1, other arithmetic, on_device(): far = jnp.sum(basis * leaf_local[..., None], 0)  2.79 us
  transfers between devices with their start and end apart: 6, of which 2 were waited for; matrix products, arithmetic and copies ran while one was open for 17% of the time, Pallas kernels for 38%

commit v1 on v0

--- a/solution.py
+++ b/solution.py
@@ -8,6 +8,7 @@
 from jax.experimental.pallas import tpu as pltpu
 from jax.sharding import PartitionSpec as P
 
+ORDER = 10
 SOFTENING = 0.01
 DELTAS = [(dx, dy, dz) for dx in (-1, 0, 1) for dy in (-1, 0, 1) for dz in (-1, 0, 1)]
 
@@ -176,114 +177,235 @@
     )(counts, padded, table)
 
 
-def translate_body(shape_info, mine, table, matrix, out, store, weights, sums, sems):
-    coef, per_device, lists, ops, wide = shape_info
+def emit_harmonics(coord_x, coord_y, coord_z, emit):
+    radius2 = coord_x * coord_x + coord_y * coord_y + coord_z * coord_z
+
+    def give(degree, azimuth, real, imag):
+        if azimuth == 0:
+            emit(degree * degree, real)
+        else:
+            emit(degree * degree + 2 * azimuth - 1, real)
+            emit(degree * degree + 2 * azimuth, imag)
+
+    top_re, top_im = jnp.ones_like(coord_x), None
+    for azimuth in range(ORDER + 1):
+        if azimuth == 1:
+            top_re, top_im = coord_x, coord_y
+        elif azimuth > 1:
+            factor = math.sqrt((2 * azimuth - 1) / (2 * azimuth))
+            top_re, top_im = (
+                factor * (coord_x * top_re - coord_y * top_im),
+                factor * (coord_x * top_im + coord_y * top_re),
+            )
+        give(azimuth, azimuth, top_re, top_im)
+        older, newer = None, (top_re, top_im)
+        for degree in range(azimuth + 1, ORDER + 1):
+            denom = math.sqrt(degree * degree - azimuth * azimuth)
+            scaled = ((2 * degree - 1) / denom) * coord_z
+            lower = None
+            if degree - 2 >= azimuth:
+                lower = (math.sqrt((degree - 1) ** 2 - azimuth * azimuth) / denom) * radius2
+            values = []
+            for part in range(1 if azimuth == 0 else 2):
+                value = scaled * newer[part]
+                if lower is not None:
+                    value = value - lower * older[part]
+                values.append(value)
+            older, newer = newer, tuple(values)
+            give(degree, azimuth, values[0], values[-1])
+
+
+def fill_basis(coords, basis):
+    leaves = coords.shape[1]
+    for first in range(0, leaves, 8):
+        rows = slice(first, first + 8)
+        x, y, z = (coords[axis, rows, :] - 0.5 for axis in range(3))
+
+        def emit(index, value):
+            basis[index, rows, :] = value
+
+        emit_harmonics(x, y, z, emit)
+
+
+def child_leaf(parent, octant, cells):
+    _, cells_y, cells_z = cells
+    half_y, half_z = cells_y // 2, cells_z // 2
+    a = parent // (half_y * half_z)
+    b = parent // half_z % half_y
+    c = parent % half_z
+    x = 2 * a + octant // 4
+    y = 2 * b + octant // 2 % 2
+    z = 2 * c + octant % 2
+    return (x * cells_y + y) * cells_z + z
+
+
+def iota(shape, dim):
+    return lax.broadcasted_iota(jnp.int32, shape, dim)
+
+
+def mask(condition):
+    return jnp.where(condition, 1.0, 0.0)
+
+
+def narrow(value):
+    return value.astype(jnp.bfloat16)
+
+
+def multiply(left, right, dims=(((1,), (0,)), ((), ()))):
+    return lax.dot_general(narrow(left), narrow(right), dims, preferred_element_type=jnp.float32)
+
+
+def multipole_body(cells, coords, charge, upward, out, basis, sums):
+    leaves, width = charge.shape
+    coef = upward.shape[1]
+    per_device = leaves // 8
+    fill_basis(coords, basis)
+    parts = jnp.concatenate(split3(charge[...]) + (jnp.zeros((128 - 3 * leaves, width)),), 0)
+    columns_all = parts.T
+    lane = iota((width, 128), 1)
+    chunk = next(n for n in range(11, 0, -1) if coef % n == 0)
+    rights = [narrow(jnp.where(lane < leaves * (3 - j), columns_all, 0.0)) for j in range(3)]
+    keep = iota((chunk, leaves, 128), 1) == iota((chunk, leaves, 128), 2) % leaves
+    for start in range(0, coef, chunk):
+        lefts = split3(basis[start : start + chunk].reshape(chunk * leaves, width))
+        result = sum(multiply(left, right) for left, right in zip(lefts, rights))
+        result = jnp.where(keep, result.reshape(chunk, leaves, 128), 0.0)
+        sums[start : start + chunk, :] = jnp.sum(result, 1)
+    folded = sums[...]
+    folded = folded + pltpu.roll(folded, 128 - leaves, 1) + pltpu.roll(folded, 128 - 2 * leaves, 1)
+    lane = iota((coef, 128), 1)
+    first, second, third = split3(folded)
+    stacked = jnp.where(lane < leaves, first, 0.0)
+    stacked = jnp.where(lane // leaves == 1, pltpu.roll(second, leaves, 1), stacked)
+    stacked = jnp.where(lane // leaves == 2, pltpu.roll(third, 2 * leaves, 1), stacked)
+    span = 128 // per_device
+    row, col = iota((128, 128), 0), iota((128, 128), 1)
+    slot = col % span
+    wanted = child_leaf(col // span, slot // 3, cells) + leaves * (slot % 3)
+    chosen = multiply(stacked, mask((row == wanted) & (slot < 24)))
+    slot = lane % span
+    result = jnp.zeros((coef, 128), jnp.float32)
+    for octant in range(8):
+        for j, left in enumerate(split3(upward[octant])):
+            right = jnp.where((slot >= 3 * octant) & (slot < 3 * octant + 3 - j), chosen, 0.0)
+            result = result + multiply(left, right)
+    out[...] = narrow(jnp.sum(result.T.reshape(per_device, span, coef), 1))
+
+
+def multipole(coords, charge, upward, cells):
+    leaves, width = charge.shape
+    coef = upward.shape[1]
+    vmem = pl.BlockSpec(memory_space=pltpu.VMEM)
+    return pl.pallas_call(
+        functools.partial(multipole_body, cells),
+        out_shape=jax.ShapeDtypeStruct((leaves // 8, coef), jnp.bfloat16),
+        in_specs=[vmem] * 3,
+        out_specs=vmem,
+        scratch_shapes=[
+            pltpu.VMEM((coef, leaves, width), jnp.float32),
+            pltpu.VMEM((coef, 128), jnp.float32),
+        ],
+        name="multipole",
+    )(coords, charge, upward)
+
+
+def translate_body(info, mine, counts, table, matrix, coords, near, downward, out, *scratch):
+    cells, per_device, lists, wide = info
+    weights, sums, basis, spread_local = scratch
+    coef, _, ops = matrix.shape
+    leaves, width = coords.shape[1:]
     rows = table.shape[0]
     span = 128 // per_device
     blocks = -(-coef // span)
-    chunk = sums.shape[0] // sems.shape[0]
-    copies = [
-        pltpu.make_async_copy(
-            matrix.at[pl.ds(chunk * index, chunk)],
-            store.at[pl.ds(chunk * index, chunk)],
-            sems.at[index],
-        )
-        for index in range(sems.shape[0])
-    ]
-    for copy in copies:
-        copy.start()
-
-    def iota(shape, dim):
-        return lax.broadcasted_iota(jnp.int32, shape, dim)
-
-    def mask(condition):
-        return jnp.where(condition, 1.0, 0.0)
+    chunk = next(n for n in range(11, 0, -1) if coef % n == 0)
+    fill_basis(coords, basis)
 
     seg = 256
     head = table[:, 0:128].astype(jnp.float32)
     owned = head[:, coef : coef + 1] + 256.0 * head[:, coef + 1 : coef + 2]
     lane = iota((rows, 128), 1)
     chosen = mask((owned.astype(jnp.int32) == lane + mine[0]) & (lane < per_device))
-    chosen = chosen.T[0:8].astype(jnp.bfloat16)
-    entries = jnp.dot(chosen, table[:, 128 : 128 + wide * seg], preferred_element_type=jnp.float32)
+    entries = multiply(chosen.T[0:8], table[:, 128 : 128 + wide * seg])
     sources = entries[:, seg : 2 * seg]
     if wide == 3:
         sources = sources + 256.0 * entries[:, 2 * seg : 3 * seg]
     sources = sources.astype(jnp.int32)
     classes = entries[:, 0:seg].astype(jnp.int32)
+    across = (((1,), (1,)), ((), ()))
     counted = []
     for row in range(per_device):
         from_cell = mask(iota((rows, seg), 0) == sources[row : row + 1])
-        to_class = mask(
-            (iota((ops, seg), 0) == classes[row : row + 1]) & (iota((ops, seg), 1) < lists)
-        )
-        counted.append(
-            lax.dot_general(
-                to_class.astype(jnp.bfloat16),
-                from_cell.astype(jnp.bfloat16),
-                (((1,), (1,)), ((), ())),
-                preferred_element_type=jnp.float32,
-            ).astype(jnp.bfloat16)
-        )
+        to_class = iota((ops, seg), 0) == classes[row : row + 1]
+        to_class = mask(to_class & (iota((ops, seg), 1) < lists))
+        counted.append(narrow(multiply(to_class, from_cell, across)))
     counted = jnp.concatenate(counted, 1)
     parents = table[:, 0:128]
-    lane = iota((rows, 128), 1)
     for block in range(blocks):
-        pick_row = iota((128, 128), 0)
-        pick_col = iota((128, 128), 1)
-        spread = mask((pick_row == span * block + pick_col % span) & (pick_row < coef))
-        tiled = jnp.dot(parents, spread.astype(jnp.bfloat16), preferred_element_type=jnp.float32)
-        stacked = jnp.concatenate(
-            [jnp.where(lane // span == row, tiled, 0.0) for row in range(per_device)], 0
-        )
-        weights[block] = jnp.dot(
-            counted, stacked.astype(jnp.bfloat16), preferred_element_type=jnp.float32
-        ).astype(jnp.bfloat16)
-    for index, copy in enumerate(copies):
-        copy.wait()
+        row, col = iota((128, 128), 0), iota((128, 128), 1)
+        tiled = multiply(parents, mask((row == span * block + col % span) & (row < coef)))
+        stacked = [jnp.where(lane // span == row, tiled, 0.0) for row in range(per_device)]
+        weights[block] = narrow(multiply(counted, jnp.concatenate(stacked, 0)))
+    for start in range(0, coef, chunk):
         total = jnp.zeros((chunk, 128), jnp.float32)
         for block in range(blocks):
             height = min(span, coef - span * block)
-            part = store[pl.ds(chunk * index, chunk), span * block : span * block + height, :]
+            part = matrix[start : start + chunk, span * block : span * block + height, :]
             if height < span:
                 fill = jnp.zeros((chunk, span - height, ops), part.dtype)
                 part = jnp.concatenate([part, fill], 1)
-            result = jnp.dot(
-                part.reshape(chunk * span, ops), weights[block], preferred_element_type=jnp.float32
-            ).reshape(chunk, span, 128)
+            result = multiply(part.reshape(chunk * span, ops), weights[block])
+            result = result.reshape(chunk, span, 128)
             keep = iota((chunk, span, 128), 1) == iota((chunk, span, 128), 2) % span
             total = total + jnp.sum(jnp.where(keep, result, 0.0), 1)
-        sums[pl.ds(chunk * index, chunk), :] = total
-    gather = mask(iota((128, 128), 0) // span == iota((128, 128), 1)).astype(jnp.bfloat16)
-    local = jnp.zeros((coef, 128), jnp.float32)
-    for piece in split3(sums[...]):
-        local = local + jnp.dot(
-            piece.astype(jnp.bfloat16), gather, preferred_element_type=jnp.float32
-        )
-    out[...] = local
-
-
-def translate(mine, table, matrix, per_device, lists, wide):
+        sums[start : start + chunk, :] = total
+    gather = mask(iota((128, 128), 0) // span == iota((128, 128), 1))
+    local = sum(multiply(piece, gather) for piece in split3(sums[...]))
+    local = jnp.concatenate(split3(local.T[0:8]), 0)
+    for octant in range(8):
+        result = jnp.zeros((8, coef), jnp.float32)
+        for j, right in enumerate(split3(downward[octant])):
+            product = multiply(local, right, across)
+            for i in range(3 - j):
+                result = result + product[8 * i : 8 * i + 8]
+        for parent in range(per_device):
+            leaf = child_leaf(parent, octant, cells)
+            spread_local[leaf : leaf + 1, 0:coef] = result[parent : parent + 1]
+    slot = iota((8, width), 1)
+    sub = iota((8, width), 0)
+    for first in range(0, leaves, 8):
+        values = spread_local[first : first + 8, :]
+        total = near[first : first + 8, :]
+        for index in range(coef):
+            column = jnp.broadcast_to(values[:, index : index + 1], (8, width))
+            total = total + column * basis[index, first : first + 8, :]
+        limit = jnp.zeros((8, width), jnp.int32)
+        for row in range(8):
+            limit = jnp.where(sub == row, counts[first + row], limit)
+        out[first : first + 8, :] = jnp.where(slot < limit, total, 0.0)
+
+
+def translate(mine, counts, table, matrix, coords, near, downward, cells, lists, wide):
     coef, _, ops = matrix.shape
-    pieces = next(n for n in range(11, 0, -1) if coef % n == 0)
+    leaves, width = near.shape
+    per_device = leaves // 8
+    span = 128 // per_device
+    smem = pl.BlockSpec(memory_space=pltpu.SMEM)
     vmem = pl.BlockSpec(memory_space=pltpu.VMEM)
-    span = 128 // per_device
     return pl.pallas_call(
-        functools.partial(translate_body, (coef, per_device, lists, ops, wide)),
-        out_shape=jax.ShapeDtypeStruct((coef, 128), jnp.float32),
-        in_specs=[pl.BlockSpec(memory_space=pltpu.SMEM), vmem, pl.BlockSpec(memory_space=pl.ANY)],
+        functools.partial(translate_body, (cells, per_device, lists, wide)),
+        out_shape=jax.ShapeDtypeStruct((leaves, width), jnp.float32),
+        in_specs=[smem, smem] + [vmem] * 5,
         out_specs=vmem,
         scratch_shapes=[
-            pltpu.VMEM(matrix.shape, matrix.dtype),
             pltpu.VMEM((-(-coef // span), ops, 128), jnp.bfloat16),
             pltpu.VMEM((coef, 128), jnp.float32),
-            pltpu.SemaphoreType.DMA((pieces,)),
+            pltpu.VMEM((coef, leaves, width), jnp.float32),
+            pltpu.VMEM((leaves, 128), jnp.float32),
         ],
         name="translate",
-    )(mine, table, matrix)
-
-
-ORDER = 10
+    )(mine, counts, table, matrix, coords, near, downward)
+
+
 MESH_AXES = ("gx", "gy", "gz")
 
 
@@ -305,49 +427,6 @@
     return value
 
 
-def harmonics(relative):
-    coord_x, coord_y, coord_z = (relative[0], relative[1], relative[2])
-    radius2 = coord_x * coord_x + coord_y * coord_y + coord_z * coord_z
-    real_part = {}
-    imag_part = {}
-    real_part[0, 0] = jnp.ones_like(coord_x)
-    imag_part[0, 0] = jnp.zeros_like(coord_x)
-    for azimuth in range(1, ORDER + 1):
-        factor = 1.0 if azimuth == 1 else math.sqrt((2 * azimuth - 1) / (2 * azimuth))
-        prev_re = real_part[azimuth - 1, azimuth - 1]
-        prev_im = imag_part[azimuth - 1, azimuth - 1]
-        real_part[azimuth, azimuth] = factor * (coord_x * prev_re - coord_y * prev_im)
-        imag_part[azimuth, azimuth] = factor * (coord_x * prev_im + coord_y * prev_re)
-    for azimuth in range(0, ORDER + 1):
-        for degree in range(azimuth + 1, ORDER + 1):
-            denom = math.sqrt(degree * degree - azimuth * azimuth)
-            first = (2 * degree - 1) / denom
-            next_re = first * coord_z * real_part[degree - 1, azimuth]
-            next_im = first * coord_z * imag_part[degree - 1, azimuth]
-            if degree - 2 >= azimuth:
-                second = math.sqrt((degree - 1) ** 2 - azimuth * azimuth) / denom
-                next_re = next_re - second * radius2 * real_part[degree - 2, azimuth]
-                next_im = next_im - second * radius2 * imag_part[degree - 2, azimuth]
-            real_part[degree, azimuth] = next_re
-            imag_part[degree, azimuth] = next_im
-    pieces = []
-    for degree in range(ORDER + 1):
-        pieces.append(real_part[degree, 0])
-        for azimuth in range(1, degree + 1):
-            pieces.append(real_part[degree, azimuth])
-            pieces.append(imag_part[degree, azimuth])
-    return pieces
-
-
-def children(field):
-    coef, size_x, size_y, size_z = field.shape
-    split = field.reshape(coef, size_x // 2, 2, size_y // 2, 2, size_z // 2, 2)
-    result = []
-    for octant in range(8):
-        result.append(split[:, :, octant // 4, :, octant // 2 % 2, :, octant % 2])
-    return result
-
-
 def columns(cell, halves, peers):
     (half_x, half_y, half_z), (_, count_y, count_z) = halves, peers
     parents_y, parents_z = half_y * count_y, half_z * count_z
@@ -375,15 +454,9 @@
     padded = extended(stacked, (("gz", 2), ("gy", 1), ("gx", 0)))
     padded = padded.reshape(-1, 4, width)
 
-    basis = jnp.stack(harmonics(offsets - 0.5), 0)
-    coef = basis.shape[0]
-    leaf_multipole = jnp.sum(basis * charge_live[None], -1)
-    parent = jnp.zeros((coef, half_x, half_y, half_z), jnp.float32)
-    for octant, child in enumerate(children(leaf_multipole)):
-        parent = parent + jnp.tensordot(
-            m2m[octant], child, axes=(1, 0), precision=lax.Precision.HIGHEST
-        )
-    parent_rows = parent.astype(jnp.bfloat16).reshape(coef, per_device).T
+    coef = m2m.shape[1]
+    coords = offsets.reshape(3, leaves, width)
+    parent_rows = multipole(coords, charge_live.reshape(leaves, width), m2m, cells)
 
     lists = list_sources.shape[1]
     wide = 2 if total_parents <= 256 else 3
@@ -407,21 +480,11 @@
     spread = jnp.broadcast_to(payload[None], (devices,) + payload.shape)
     table = lax.all_to_all(spread, MESH_AXES, 0, 0).reshape(total_parents, payload.shape[1])
 
-    near = near_field(counts.reshape(-1), padded, cells).reshape(charges.shape)
-
+    flat_counts = counts.reshape(-1)
+    near = near_field(flat_counts, padded, cells)
     mine = (lax.axis_index(MESH_AXES) * per_device).astype(jnp.int32).reshape(1)
-    local = translate(mine, table, m2l, per_device, lists, wide)
-    parent_local = local[:, :per_device].reshape(coef, half_x, half_y, half_z)
-    pieces = [
-        jnp.tensordot(l2l[octant], parent_local, axes=(1, 0), precision=lax.Precision.HIGHEST)
-        for octant in range(8)
-    ]
-    joined = jnp.stack(pieces, 0).reshape((2, 2, 2, coef, half_x, half_y, half_z))
-    leaf_local = jnp.transpose(joined, (3, 4, 0, 5, 1, 6, 2)).reshape(
-        coef, cells_x, cells_y, cells_z
-    )
-    far = jnp.sum(basis * leaf_local[..., None], 0)
-    return live * (near + far)
+    result = translate(mine, flat_counts, table, m2l, coords, near, l2l, cells, lists, wide)
+    return result.reshape(charges.shape)
 
 
 def solution(mesh):

time: 95.7 us -> 89.7 us (0.937)
  the two profiles are of different devices: /device:TPU:18 before, /device:TPU:2 now
where the time goes in v1:
time: 89.7 us; the launch traced here: 88.5 us
  Pallas kernels  49 us (55%)
  starting transfers between devices  18.1 us (20%)
  local copies, waits for them, and re-layouts  13.2 us (15%)
  other arithmetic  4.17 us (5%)
  waiting for transfers between devices  3.91 us (4%)
    pallas_call x1, Pallas kernels, near_field(): pl.pallas_call(functools.partial(near_body, cells), out_shape=jax.ShapeDt...  34.7 us
    pallas_call x1, Pallas kernels, translate(): pl.pallas_call(functools.partial(translate_body, (cells, per_device, list...  9.26 us
    all_to_all x1, starting transfers between devices, on_device(): lax.all_to_all(spread, MESH_AXES, 0, 0)  6.13 us
    ppermute x2, starting transfers between devices, extended(): before = lax.ppermute(last, axis, up)  5.3 us
    ppermute x2, starting transfers between devices, extended(): after = lax.ppermute(leading, axis, [(j, i) for i, j in up])  5.11 us
    pallas_call x1, Pallas kernels, multipole(): pl.pallas_call(functools.partial(multipole_body, cells), out_shape=jax.Sh...  4.95 us
    unnamed x3, local copies, waits for them, and re-layouts  3.95 us
    ppermute x2, waiting for transfers between devices, extended(): after = lax.ppermute(leading, axis, [(j, i) for i, j in up])  3.77 us
  transfers between devices with their start and end apart: 6, of which 2 were waited for; matrix products, arithmetic and copies ran while one was open for 15% of the time, Pallas kernels for 45%

profile of v1, /device:TPU:2, one launch (start us, length us, event | category | flops | bytes accessed | tf_op | source)
XLA Modules:
  0.0 88.5 jit_solution(15717521192768858197)
XLA Ops:
  0.0 0.8 slice_bitcast_fusion.2
  0.8 0.8 fusion.26
  1.7 1.6 %collective-permute-start = (f32[2,4,1,4,256]{4,2,1,0,3:T(1,128)S(1)}, f32[2,4,1,4,256]{4,2,1,0,3:T(1,128)S(1)}, u32[]{:S(2)}, u32[]{:S(2)}) collective-permute-start(f32[2,4,1,4,256]{4,2,1,0,3:T(1,128)S(1)} %broadcast_select_fusion.2), channel_id=1, source_target_pairs={{0,1},{1,0},{2,3},{3,2},{4,5},{5,4},{6,7},{7,6},{8,9},{9,8},{10,11... | collective-permute-start | bytes 98312 | tf_op jit(solution)/shard_map/ppermute | solution.py:419
  3.3 0.8 fusion
  4.1 0.7 fusion.12
  4.9 0.7 convert_bitcast_fusion
  5.8 1.9 %collective-permute-start.1 = (f32[2,1,6,4,256]{4,2,1,0,3:T(8,128)S(1)}, f32[2,1,6,4,256]{4,2,1,0,3:T(8,128)S(1)}, u32[]{:S(2)}, u32[]{:S(2)}) collective-permute-start(f32[2,1,6,4,256]{4,2,1,0,3:T(8,128)S(1)} %get-tuple-element.9), channel_id=1, source_target_pairs={{0,2},{2,4},{4,6},{1,3},{3,5},{5,7},{8,10},{10,12},{12,14},{9,11},... | collective-permute-start | bytes 147464 | tf_op jit(solution)/shard_map/ppermute | solution.py:424
  7.7 3.6 %collective-permute-start.2 = (f32[2,1,6,4,256]{4,2,1,0,3:T(8,128)S(1)}, f32[2,1,6,4,256]{4,2,1,0,3:T(8,128)S(1)}, u32[]{:S(2)}, u32[]{:S(2)}) collective-permute-start(f32[2,1,6,4,256]{4,2,1,0,3:T(8,128)S(1)} %get-tuple-element.10), channel_id=1, source_target_pairs={{2,0},{4,2},{6,4},{3,1},{5,3},{7,5},{10,8},{12,10},{14,12},{11,9},... | collective-permute-start | bytes 147464 | tf_op jit(solution)/shard_map/ppermute | solution.py:425
  11.4 1.6 %reshape.51.coords = f32[3,32,256]{2,1,0:T(8,128)} reshape(f32[3,2,4,4,256]{4,3,2,1,0:T(4,128)} %param.10) | data formatting | bytes 196608 | tf_op jit(solution)/shard_map/reshape | solution.py:458
  12.9 1.9 %copy.11.upward = f32[8,121,121]{2,1,0:T(8,128)} copy(f32[8,121,121]{2,0,1:T(8,128)} %param.16) | data formatting | bytes 937024 | tf_op args[6]
  16.4 5.0 %multipole.1 = bf16[4,121]{1,0:T(4,128)(2,1)} custom-call(f32[3,32,256]{2,1,0:T(8,128)} %reshape.51.coords, f32[32,256]{1,0:T(8,128)} %reshape.52.charge, f32[8,121,121]{2,1,0:T(8,128)} %copy.11.upward), custom_call_target="tpu_custom_call" | custom-call | tf_op jit(solution)/shard_map/multipole/pallas_call | solution.py:299
  21.4 0.7 concatenate.12
  22.1 0.7 broadcast_in_dim.8
  22.8 6.1 %all-to-all-start = ((bf16[32,4,640]{2,1,0:T(4,128)(2,1)}), bf16[32,4,640]{2,1,0:T(4,128)(2,1)S(1)}, u32[]{:S(2)}, u32[]{:S(2)}) async-start(bf16[32,4,640]{2,1,0:T(4,128)(2,1)} %broadcast_in_dim.8), calls=%async_computation | async-start | bytes 327680 | tf_op jit(solution)/shard_map/all_to_all | solution.py:481
  29.1 3.4 %collective-permute-start.3 = (f32[1,6,6,4,256]{4,2,1,0,3:T(8,128)S(1)}, f32[1,6,6,4,256]{4,2,1,0,3:T(8,128)S(1)}, u32[]{:S(2)}, u32[]{:S(2)}) collective-permute-start(f32[1,6,6,4,256]{4,2,1,0,3:T(8,128)S(1)} %get-tuple-element.7), channel_id=1, source_target_pairs={{0,8},{8,16},{16,24},{1,9},{9,17},{17,25},{2,10},{10,18},{18,26},{... | collective-permute-start | bytes 442376 | tf_op jit(solution)/shard_map/ppermute | solution.py:424
  32.5 1.5 %collective-permute-start.4 = (f32[1,6,6,4,256]{4,2,1,0,3:T(8,128)S(1)}, f32[1,6,6,4,256]{4,2,1,0,3:T(8,128)S(1)}, u32[]{:S(2)}, u32[]{:S(2)}) collective-permute-start(f32[1,6,6,4,256]{4,2,1,0,3:T(8,128)S(1)} %get-tuple-element.8), channel_id=1, source_target_pairs={{8,0},{16,8},{24,16},{9,1},{17,9},{25,17},{10,2},{18,10},{26,18},{... | collective-permute-start | bytes 442376 | tf_op jit(solution)/shard_map/ppermute | solution.py:425
  34.0 1.4 %reshape.50.counts = s32[32]{0:T(128)} reshape(s32[2,4,4]{2,1,0:T(4,128)} %param.12) | data formatting | bytes 256 | tf_op jit(solution)/shard_map/reshape | solution.py:483
  35.3 1.9 %copy.15.downward = f32[8,121,121]{2,1,0:T(8,128)} copy(f32[8,121,121]{2,0,1:T(8,128)} %param.18) | data formatting | bytes 937024 | tf_op args[8]
  37.3 3.8 %collective-permute-done.4 = f32[1,6,6,4,256]{4,2,1,0,3:T(8,128)S(1)} collective-permute-done((f32[1,6,6,4,256]{4,2,1,0,3:T(8,128)S(1)}, f32[1,6,6,4,256]{4,2,1,0,3:T(8,128)S(1)}, u32[]{:S(2)}, u32[]{:S(2)}) %collective-permute-start.4) | collective-permute-done | bytes 147488 | tf_op jit(solution)/shard_map/ppermute | solution.py:425
  41.2 1.2 %copy.14 = f32[4,6,6,4,256]{4,3,2,1,0:T(4,128)} copy(f32[4,6,6,4,256]{4,2,1,0,3:T(8,128)S(1)} %pad_maximum_fusion) | data formatting | bytes 1179648 | tf_op jit(solution)/shard_map/concatenate | solution.py:426
  42.4 34.7 %near.1 = f32[32,256]{1,0:T(8,128)} custom-call(s32[32]{0:T(128)} %reshape.50.counts, f32[144,4,256]{2,1,0:T(4,128)} %bitcast.14, bf16[27,64,128]{2,1,0:T(8,128)(2,1)} %constant.215.clone.table), custom_call_target="tpu_custom_call" | custom-call | tf_op jit(solution)/shard_map/near/pallas_call | solution.py:166
  77.1 0.7 reshape.53.table
  77.8 9.3 %translate.1 = f32[32,256]{1,0:T(8,128)} custom-call(s32[1]{0:T(128)} %bitcast.mine, s32[32]{0:T(128)} %reshape.50.counts, bf16[128,640]{1,0:T(8,128)(2,1)} %reshape.53.table, bf16[121,121,256]{2,1,0:T(8,128)(2,1)} %matrix.1, f32[3,32,256]{2,1,0:T(8,128)} %reshape.51.coords, f32[32,256]{1,0:T(8,128)} %near.1, f32[8,121,121]{2,1,0:T(8,128)} %copy.15.downward), custom_call_target="tpu_custom_call" | custom-call | tf_op jit(solution)/shard_map/translate/pallas_call | solution.py:394
  87.1 1.4 %reshape.55 = f32[2,4,4,256]{3,2,1,0:T(4,128)} reshape(f32[32,256]{1,0:T(8,128)} %translate.1) | data formatting | bytes 65536 | tf_op jit(solution)/shard_map/reshape | solution.py:487
  (19 shorter events, 2.1 us)
Async XLA Ops:
  1.7 4.0 %collective-permute-start = (f32[2,4,1,4,256]{4,2,1,0,3:T(1,128)S(1)}, f32[2,4,1,4,256]{4,2,1,0,3:T(1,128)S(1)}, u32[]{:S(2)}, u32[]{:S(2)}) collective-permute-start(f32[2,4,1,4,256]{4,2,1,0,3:T(1,128)S(1)} %broadcast_select_fusion.2), channel_id=1, source_target_pairs={{0,1},{1,0},{2,3},{3,2},{4,5},{5,4},{6,7},{7,6},{8,9},{9,8},{10,11... | collective-permute-start | bytes 98312 | tf_op jit(solution)/shard_map/ppermute | solution.py:419
  5.8 23.2 %collective-permute-start.1 = (f32[2,1,6,4,256]{4,2,1,0,3:T(8,128)S(1)}, f32[2,1,6,4,256]{4,2,1,0,3:T(8,128)S(1)}, u32[]{:S(2)}, u32[]{:S(2)}) collective-permute-start(f32[2,1,6,4,256]{4,2,1,0,3:T(8,128)S(1)} %get-tuple-element.9), channel_id=1, source_target_pairs={{0,2},{2,4},{4,6},{1,3},{3,5},{5,7},{8,10},{10,12},{12,14},{9,11},... | collective-permute-start | bytes 147464 | tf_op jit(solution)/shard_map/ppermute | solution.py:424
  7.7 21.3 %collective-permute-start.2 = (f32[2,1,6,4,256]{4,2,1,0,3:T(8,128)S(1)}, f32[2,1,6,4,256]{4,2,1,0,3:T(8,128)S(1)}, u32[]{:S(2)}, u32[]{:S(2)}) collective-permute-start(f32[2,1,6,4,256]{4,2,1,0,3:T(8,128)S(1)} %get-tuple-element.10), channel_id=1, source_target_pairs={{2,0},{4,2},{6,4},{3,1},{5,3},{7,5},{10,8},{12,10},{14,12},{11,9},... | collective-permute-start | bytes 147464 | tf_op jit(solution)/shard_map/ppermute | solution.py:425
  22.8 54.3 %all-to-all-start = ((bf16[32,4,640]{2,1,0:T(4,128)(2,1)}), bf16[32,4,640]{2,1,0:T(4,128)(2,1)S(1)}, u32[]{:S(2)}, u32[]{:S(2)}) async-start(bf16[32,4,640]{2,1,0:T(4,128)(2,1)} %broadcast_in_dim.8), calls=%async_computation | async-start | bytes 327680 | tf_op jit(solution)/shard_map/all_to_all | solution.py:481
  29.1 8.2 %collective-permute-start.3 = (f32[1,6,6,4,256]{4,2,1,0,3:T(8,128)S(1)}, f32[1,6,6,4,256]{4,2,1,0,3:T(8,128)S(1)}, u32[]{:S(2)}, u32[]{:S(2)}) collective-permute-start(f32[1,6,6,4,256]{4,2,1,0,3:T(8,128)S(1)} %get-tuple-element.7), channel_id=1, source_target_pairs={{0,8},{8,16},{16,24},{1,9},{9,17},{17,25},{2,10},{10,18},{18,26},{... | collective-permute-start | bytes 442376 | tf_op jit(solution)/shard_map/ppermute | solution.py:424
  32.5 8.5 %collective-permute-start.4 = (f32[1,6,6,4,256]{4,2,1,0,3:T(8,128)S(1)}, f32[1,6,6,4,256]{4,2,1,0,3:T(8,128)S(1)}, u32[]{:S(2)}, u32[]{:S(2)}) collective-permute-start(f32[1,6,6,4,256]{4,2,1,0,3:T(8,128)S(1)} %get-tuple-element.8), channel_id=1, source_target_pairs={{8,0},{16,8},{24,16},{9,1},{17,9},{25,17},{10,2},{18,10},{26,18},{... | collective-permute-start | bytes 442376 | tf_op jit(solution)/shard_map/ppermute | solution.py:425

commit v2 on v1

v2 whole, which is shorter than its diff:
```python
import math
import functools
import numpy as np
import jax
import jax.numpy as jnp
from jax import lax
from jax.experimental import pallas as pl
from jax.experimental.pallas import tpu as pltpu
from jax.sharding import PartitionSpec as P


ORDER = 10
SOFTENING = 0.01
DELTAS = [(dx, dy, dz) for dx in (-1, 0, 1) for dy in (-1, 0, 1) for dz in (-1, 0, 1)]
DEPTH = 80


def delta_tables():
    table = np.zeros((27, 32, 128), np.float32)
    for index, delta in enumerate(DELTAS):
        for axis in range(3):
            for group in range(3):
                table[index, 3 * group + axis] = 2.0 * delta[axis]
                table[index, 16 + 3 * group + axis] = delta[axis]
        rest = np.float32(sum(d * d for d in delta) + SOFTENING)
        for part in range(3):
            piece = np.asarray(rest).astype(jnp.bfloat16).astype(np.float32)
            table[index, 25 + part] = piece
            rest = np.float32(rest - piece)
    return table


def expand_table():
    table = np.zeros((16, 128), np.float32)
    for axis in range(3):
        first, second, third = axis, 3 + axis, 6 + axis
        for group in range(3):
            table[first, 3 * group + axis] = -2.0
            table[12, 48 + 3 * group + axis] = 1.0
        for group in range(2):
            table[second, 16 + 3 * group + axis] = -2.0
        table[third, 32 + axis] = -2.0
        table[12, 9 + axis] = 1.0
        table[9 + axis, 12 + axis] = 1.0
        for group, source in enumerate((first, second, third)):
            table[source, 64 + 3 * group + axis] = -2.0
        table[12, 73 + axis] = 1.0
    return table


def split3(value):
    first = value.astype(jnp.bfloat16).astype(jnp.float32)
    rest = value - first
    second = rest.astype(jnp.bfloat16).astype(jnp.float32)
    third = (rest - second).astype(jnp.bfloat16).astype(jnp.float32)
    return first, second, third


def iota(shape, dim):
    return lax.broadcasted_iota(jnp.int32, shape, dim)


def mask(condition):
    return jnp.where(condition, 1.0, 0.0)


def narrow(value):
    return value.astype(jnp.bfloat16)


def multiply(left, right, dims=(((1,), (0,)), ((), ()))):
    return lax.dot_general(narrow(left), narrow(right), dims, preferred_element_type=jnp.float32)


def near_body(cells, counts, source, table, expand, out, rows32, base, left, total):
    cells_x, cells_y, cells_z = cells
    _, pad_x, pad_y, pad_z, width = source.shape
    leaves = cells_x * cells_y * cells_z
    tiles = width // 128
    sources = pad_x * pad_y * pad_z

    def fill(column, carry):
        a, b = column // pad_y, column % pad_y
        parts, norm = [], 0.0
        for axis in range(3):
            centred = source[axis, a, b] - 0.5
            norm = norm + centred * centred
            parts.append(split3(centred))
        rows = [parts[axis][part] for part in range(3) for axis in range(3)]
        rows += list(split3(norm)) + [jnp.ones_like(norm)] * 3 + [source[3, a, b]]
        for index, row in enumerate(rows):
            for part in range(tiles):
                start = part * sources * 16 + column * pad_z * 16 + index
                rows32[pl.ds(start, pad_z, stride=16), :] = row[:, 128 * part : 128 * part + 128]
        return carry

    def pack(leaf, carry):
        for part in range(tiles):
            start = pl.multiple_of((part * sources + leaf) * 16, 16)
            base[leaf, :, 128 * part : 128 * part + 128] = narrow(rows32[pl.ds(start, 16), :])
        return carry

    lax.fori_loop(0, pad_x * pad_y, fill, 0)
    lax.fori_loop(0, pad_x * pad_y * pad_z, pack, 0, unroll=8)

    def place(leaf):
        return leaf // (cells_y * cells_z), leaf // cells_z % cells_y, leaf % cells_z

    def home(leaf):
        a, b, c = place(leaf)
        return ((a + 1) * pad_y + b + 1) * pad_z + c + 1

    def count_of(leaf):
        a, b, c = place(leaf)
        return counts[a, b, c]

    def fill_left(leaf):
        features = base[home(leaf)].astype(jnp.float32).T
        left[leaf % 2] = narrow(multiply(features, expand[...]))

    ones = jnp.ones((8, 128), jnp.bfloat16)
    across = (((1,), (1,)), ((), ()))

    def finish(leaf):
        result = sum(multiply(ones, piece, across) for piece in split3(total[leaf % 2]))
        slot = iota((1, width), 1)
        out[pl.ds(leaf, 1), :] = jnp.where(slot < count_of(leaf), result[0:1], 0.0)

    def block(leaf, height):
        centre = home(leaf)
        lhs = left[leaf % 2, 0:height, 0:DEPTH]
        acc = jnp.zeros((height, 128), jnp.float32)
        for index, (dx, dy, dz) in enumerate(DELTAS):
            other = centre + (dx * pad_y + dy) * pad_z + dz
            scale = table[index, 0:16]
            fixed = table[index, 16:32]
            halves = []
            for part in range(tiles):
                feature = base[other, :, 128 * part : 128 * part + 128]
                halves.append(
                    jnp.concatenate([feature, feature, feature, feature * scale, fixed], 0)
                )
            rhs = jnp.concatenate(halves, 1)
            dist2 = jnp.dot(lhs, rhs, preferred_element_type=jnp.float32)
            inverse = lax.rsqrt(dist2)
            if dx == 0 and dy == 0 and dz == 0:
                inverse = jnp.where(iota(inverse.shape, 0) == iota(inverse.shape, 1), 0.0, inverse)
            for part in range(tiles):
                amount = rows32[pl.ds((part * sources + other) * 16 + 15, 1), :]
                acc = acc + inverse[:, 128 * part : 128 * part + 128] * amount
        fill_left(jnp.minimum(leaf + 1, leaves - 1))
        finish(jnp.maximum(leaf - 1, 0))
        total[leaf % 2, 0:height] = acc

    fill_left(0)
    total[...] = jnp.zeros_like(total)
    step = 32

    def choose(leaf, pieces, low, high):
        if high - low == 1:
            block(leaf, high * step)
            return
        middle = (low + high) // 2
        pl.when(pieces <= middle)(lambda: choose(leaf, pieces, low, middle))
        pl.when(pieces > middle)(lambda: choose(leaf, pieces, middle, high))

    def leaf_step(leaf, carry):
        pieces = (count_of(leaf) + step - 1) // step
        choose(leaf, pieces, 0, width // step)
        return carry

    lax.fori_loop(0, leaves, leaf_step, 0)
    finish(leaves - 1)


def near_field(counts, padded, cells):
    leaves = cells[0] * cells[1] * cells[2]
    width = padded.shape[-1]
    sources = padded.shape[1] * padded.shape[2] * padded.shape[3]
    table = jnp.asarray(delta_tables(), jnp.bfloat16)
    expand = jnp.asarray(expand_table(), jnp.bfloat16)
    vmem = pl.BlockSpec(memory_space=pltpu.VMEM)
    return pl.pallas_call(
        functools.partial(near_body, cells),
        out_shape=jax.ShapeDtypeStruct((leaves, width), jnp.float32),
        in_specs=[pl.BlockSpec(memory_space=pltpu.SMEM)] + [vmem] * 3,
        out_specs=vmem,
        scratch_shapes=[
            pltpu.VMEM((sources * 16 * (width // 128), 128), jnp.float32),
            pltpu.VMEM((sources, 16, width), jnp.bfloat16),
            pltpu.VMEM((2, width, 128), jnp.bfloat16),
            pltpu.VMEM((2, width, 128), jnp.float32),
        ],
        name="near",
    )(counts, padded, table, expand)


def emit_harmonics(coord_x, coord_y, coord_z, emit):
    radius2 = coord_x * coord_x + coord_y * coord_y + coord_z * coord_z

    def give(degree, azimuth, real, imag):
        if azimuth == 0:
            emit(degree * degree, real)
        else:
            emit(degree * degree + 2 * azimuth - 1, real)
            emit(degree * degree + 2 * azimuth, imag)

    top_re, top_im = jnp.ones_like(coord_x), None
    for azimuth in range(ORDER + 1):
        if azimuth == 1:
            top_re, top_im = coord_x, coord_y
        elif azimuth > 1:
            factor = math.sqrt((2 * azimuth - 1) / (2 * azimuth))
            top_re, top_im = (
                factor * (coord_x * top_re - coord_y * top_im),
                factor * (coord_x * top_im + coord_y * top_re),
            )
        give(azimuth, azimuth, top_re, top_im)
        older, newer = None, (top_re, top_im)
        for degree in range(azimuth + 1, ORDER + 1):
            denom = math.sqrt(degree * degree - azimuth * azimuth)
            scaled = ((2 * degree - 1) / denom) * coord_z
            lower = None
            if degree - 2 >= azimuth:
                lower = (math.sqrt((degree - 1) ** 2 - azimuth * azimuth) / denom) * radius2
            values = []
            for part in range(1 if azimuth == 0 else 2):
                value = scaled * newer[part]
                if lower is not None:
                    value = value - lower * older[part]
                values.append(value)
            older, newer = newer, tuple(values)
            give(degree, azimuth, values[0], values[-1])


def flatten(field, flat):
    size_x, size_y, size_z = field.shape[:3]
    for a in range(size_x):
        for b in range(size_y):
            first = (a * size_y + b) * size_z
            flat[first : first + size_z, :] = field[a, b]


def fill_basis(offsets, flat, basis):
    leaves = flat.shape[1]
    for axis in range(3):
        flatten(offsets.at[axis], flat.at[axis])
    for first in range(0, leaves, 8):
        rows = slice(first, first + 8)
        x, y, z = (flat[axis, rows, :] - 0.5 for axis in range(3))

        def emit(index, value):
            basis[index, rows, :] = value

        emit_harmonics(x, y, z, emit)


def child_leaf(parent, octant, cells):
    _, cells_y, cells_z = cells
    half_y, half_z = cells_y // 2, cells_z // 2
    a = parent // (half_y * half_z)
    b = parent // half_z % half_y
    c = parent % half_z
    x = 2 * a + octant // 4
    y = 2 * b + octant // 2 % 2
    z = 2 * c + octant % 2
    return (x * cells_y + y) * cells_z + z


def multipole_body(cells, offsets, charges, upward, out, flat, charge, basis, sums):
    leaves, width = charge.shape
    coef = upward.shape[0]
    per_device = leaves // 8
    flatten(charges, charge)
    fill_basis(offsets, flat, basis)
    parts = jnp.concatenate(split3(charge[...]) + (jnp.zeros((128 - 3 * leaves, width)),), 0)
    columns_all = parts.T
    lane = iota((width, 128), 1)
    chunk = next(n for n in range(11, 0, -1) if coef % n == 0)
    rights = [narrow(jnp.where(lane < leaves * (3 - j), columns_all, 0.0)) for j in range(3)]
    keep = iota((chunk, leaves, 128), 1) == iota((chunk, leaves, 128), 2) % leaves
    for start in range(0, coef, chunk):
        lefts = split3(basis[start : start + chunk].reshape(chunk * leaves, width))
        result = sum(multiply(left, right) for left, right in zip(lefts, rights))
        result = jnp.where(keep, result.reshape(chunk, leaves, 128), 0.0)
        sums[start : start + chunk, :] = jnp.sum(result, 1)
    folded = sums[...]
    folded = folded + pltpu.roll(folded, 128 - leaves, 1) + pltpu.roll(folded, 128 - 2 * leaves, 1)
    lane = iota((coef, 128), 1)
    first, second, third = split3(folded)
    stacked = jnp.where(lane < leaves, first, 0.0)
    stacked = jnp.where(lane // leaves == 1, pltpu.roll(second, leaves, 1), stacked)
    stacked = jnp.where(lane // leaves == 2, pltpu.roll(third, 2 * leaves, 1), stacked)
    span = 128 // per_device
    row, col = iota((128, 128), 0), iota((128, 128), 1)
    slot = col % span
    wanted = child_leaf(col // span, slot // 3, cells) + leaves * (slot % 3)
    chosen = multiply(stacked, mask((row == wanted) & (slot < 24)))
    slot = lane % span
    result = jnp.zeros((coef, 128), jnp.float32)
    for octant in range(8):
        for j, left in enumerate(split3(upward[:, octant, :])):
            right = jnp.where((slot >= 3 * octant) & (slot < 3 * octant + 3 - j), chosen, 0.0)
            result = result + multiply(left, right)
    out[...] = narrow(jnp.sum(result.T.reshape(per_device, span, coef), 1))


def multipole(offsets, charge_live, upward):
    cells, width = charge_live.shape[:3], charge_live.shape[3]
    leaves = cells[0] * cells[1] * cells[2]
    coef = upward.shape[0]
    vmem = pl.BlockSpec(memory_space=pltpu.VMEM)
    return pl.pallas_call(
        functools.partial(multipole_body, cells),
        out_shape=jax.ShapeDtypeStruct((leaves // 8, coef), jnp.bfloat16),
        in_specs=[vmem] * 3,
        out_specs=vmem,
        scratch_shapes=[
            pltpu.VMEM((3, leaves, width), jnp.float32),
            pltpu.VMEM((leaves, width), jnp.float32),
            pltpu.VMEM((coef, leaves, width), jnp.float32),
            pltpu.VMEM((coef, 128), jnp.float32),
        ],
        name="multipole",
    )(offsets, charge_live, upward)


def translate_body(info, mine, counts, table, remote, offsets, near, downward, out, *scratch):
    cells, per_device, lists, wide = info
    matrix, weights, sums, flat, basis, spread_local, sem = scratch
    fetch = pltpu.make_async_copy(remote, matrix, sem)
    fetch.start()
    coef, _, ops = matrix.shape
    leaves, width = near.shape
    _, cells_y, cells_z = cells
    rows = table.shape[0]
    span = 128 // per_device
    blocks = -(-coef // span)
    chunk = next(n for n in range(11, 0, -1) if coef % n == 0)
    fill_basis(offsets, flat, basis)

    seg = 256
    head = table[:, 0:128].astype(jnp.float32)
    owned = head[:, coef : coef + 1] + 256.0 * head[:, coef + 1 : coef + 2]
    lane = iota((rows, 128), 1)
    chosen = mask((owned.astype(jnp.int32) == lane + mine[0]) & (lane < per_device))
    entries = multiply(chosen.T[0:8], table[:, 128 : 128 + wide * seg])
    sources = entries[:, seg : 2 * seg]
    if wide == 3:
        sources = sources + 256.0 * entries[:, 2 * seg : 3 * seg]
    sources = sources.astype(jnp.int32)
    classes = entries[:, 0:seg].astype(jnp.int32)
    across = (((1,), (1,)), ((), ()))
    counted = []
    for row in range(per_device):
        from_cell = mask(iota((rows, seg), 0) == sources[row : row + 1])
        to_class = iota((ops, seg), 0) == classes[row : row + 1]
        to_class = mask(to_class & (iota((ops, seg), 1) < lists))
        counted.append(narrow(multiply(to_class, from_cell, across)))
    counted = jnp.concatenate(counted, 1)
    parents = table[:, 0:128]
    for block in range(blocks):
        row, col = iota((128, 128), 0), iota((128, 128), 1)
        tiled = multiply(parents, mask((row == span * block + col % span) & (row < coef)))
        stacked = [jnp.where(lane // span == row, tiled, 0.0) for row in range(per_device)]
        weights[block] = narrow(multiply(counted, jnp.concatenate(stacked, 0)))
    fetch.wait()
    for start in range(0, coef, chunk):
        total = jnp.zeros((chunk, 128), jnp.float32)
        for block in range(blocks):
            height = min(span, coef - span * block)
            part = matrix[start : start + chunk, span * block : span * block + height, :]
            if height < span:
                fill = jnp.zeros((chunk, span - height, ops), part.dtype)
                part = jnp.concatenate([part, fill], 1)
            result = multiply(part.reshape(chunk * span, ops), weights[block])
            result = result.reshape(chunk, span, 128)
            keep = iota((chunk, span, 128), 1) == iota((chunk, span, 128), 2) % span
            total = total + jnp.sum(jnp.where(keep, result, 0.0), 1)
        sums[start : start + chunk, :] = total
    gather = mask(iota((128, 128), 0) // span == iota((128, 128), 1))
    local = sum(multiply(piece, gather) for piece in split3(sums[...]))
    local = jnp.concatenate(split3(local.T[0:8]), 0)
    for octant in range(8):
        result = jnp.zeros((8, coef), jnp.float32)
        for j, right in enumerate(split3(downward[:, octant, :])):
            product = multiply(local, right, across)
            for i in range(3 - j):
                result = result + product[8 * i : 8 * i + 8]
        for parent in range(per_device):
            leaf = child_leaf(parent, octant, cells)
            spread_local[leaf : leaf + 1, 0:coef] = result[parent : parent + 1]
    slot = iota((8, width), 1)
    sub = iota((8, width), 0)
    for first in range(0, leaves, 8):
        values = spread_local[first : first + 8, :]
        total = near[first : first + 8, :]
        for index in range(coef):
            column = jnp.broadcast_to(values[:, index : index + 1], (8, width))
            total = total + column * basis[index, first : first + 8, :]
        limit = jnp.zeros((8, width), jnp.int32)
        for row in range(8):
            leaf = first + row
            count = counts[leaf // (cells_y * cells_z), leaf // cells_z % cells_y, leaf % cells_z]
            limit = jnp.where(sub == row, count, limit)
        total = jnp.where(slot < limit, total, 0.0)
        for row in range(0, 8, cells_z):
            leaf = first + row
            a, b = leaf // (cells_y * cells_z), leaf // cells_z % cells_y
            out[a, b] = total[row : row + cells_z]


def translate(mine, counts, table, matrix, offsets, near, downward, lists, wide):
    cells = counts.shape
    coef, _, ops = matrix.shape
    leaves, width = near.shape
    per_device = leaves // 8
    span = 128 // per_device
    smem = pl.BlockSpec(memory_space=pltpu.SMEM)
    vmem = pl.BlockSpec(memory_space=pltpu.VMEM)
    return pl.pallas_call(
        functools.partial(translate_body, (cells, per_device, lists, wide)),
        out_shape=jax.ShapeDtypeStruct(cells + (width,), jnp.float32),
        in_specs=[smem, smem, vmem, pl.BlockSpec(memory_space=pl.ANY)] + [vmem] * 3,
        out_specs=vmem,
        scratch_shapes=[
            pltpu.VMEM(matrix.shape, matrix.dtype),
            pltpu.VMEM((-(-coef // span), ops, 128), jnp.bfloat16),
            pltpu.VMEM((coef, 128), jnp.float32),
            pltpu.VMEM((3, leaves, width), jnp.float32),
            pltpu.VMEM((coef, leaves, width), jnp.float32),
            pltpu.VMEM((leaves, 128), jnp.float32),
            pltpu.SemaphoreType.DMA(()),
        ],
        name="translate",
    )(mine, counts, table, matrix, offsets, near, downward)


MESH_AXES = ("gx", "gy", "gz")


def extended(value, sides):
    for axis, dim in sides:
        value = padded_along(value, axis, dim)
    return value


def padded_along(value, axis, dim):
    peers, length = lax.axis_size(axis), value.shape[dim]
    last = lax.slice_in_dim(value, length - 1, length, axis=dim)
    leading = lax.slice_in_dim(value, 0, 1, axis=dim)
    if peers == 2:
        upper = lax.axis_index(axis) == 1
        other = lax.ppermute(jnp.where(upper, leading, last), axis, [(0, 1), (1, 0)])
        before = jnp.where(upper, other, 0.0)
        after = jnp.where(upper, 0.0, other)
    else:
        up = [(i, i + 1) for i in range(peers - 1)]
        before = lax.ppermute(last, axis, up)
        after = lax.ppermute(leading, axis, [(j, i) for i, j in up])
    return jnp.concatenate([before, value, after], axis=dim)


def columns(cell, halves, peers):
    (half_x, half_y, half_z), (_, count_y, count_z) = halves, peers
    parents_y, parents_z = half_y * count_y, half_z * count_z
    cell_a = cell // (parents_y * parents_z)
    cell_b = cell // parents_z % parents_y
    cell_c = cell % parents_z
    device = (cell_a // half_x * count_y + cell_b // half_y) * count_z + cell_c // half_z
    local = (cell_a % half_x * half_y + cell_b % half_y) * half_z + cell_c % half_z
    return device * (half_x * half_y * half_z) + local


def per_block(offsets, charges, counts, owned_cell, list_sources, list_ops, m2m, m2l, l2l):
    cells = cells_x, cells_y, cells_z = charges.shape[:3]
    width = charges.shape[3]
    halves = half_x, half_y, half_z = (cells_x // 2, cells_y // 2, cells_z // 2)
    per_device = half_x * half_y * half_z
    peers = tuple(lax.axis_size(axis) for axis in MESH_AXES)
    devices = peers[0] * peers[1] * peers[2]
    total_parents = per_device * devices
    slot_ids = jnp.arange(width, dtype=jnp.int32)
    live = (slot_ids[None, None, None, :] < counts[..., None]).astype(jnp.float32)
    charge_live = charges * live
    stacked = jnp.concatenate([offsets, charge_live[None]], 0)
    padded = extended(stacked, (("gz", 3), ("gy", 2), ("gx", 1)))

    coef = m2m.shape[1]
    parent_rows = multipole(offsets, charge_live, m2m.transpose(1, 0, 2))

    lists = list_sources.shape[1]
    wide = 2 if total_parents <= 256 else 3
    owner_columns = columns(owned_cell, halves, peers)[:, None]
    source_columns = columns(list_sources, halves, peers)

    def segment(values, size):
        values = values.astype(jnp.bfloat16)
        return jnp.pad(values, ((0, 0), (0, size - values.shape[1])))

    pieces = [
        parent_rows,
        segment(owner_columns % 256, 1),
        segment(owner_columns // 256, 127 - coef),
        segment(list_ops, 256),
        segment(source_columns % 256, 256),
    ]
    if wide == 3:
        pieces.append(segment(source_columns // 256, 256))
    payload = jnp.concatenate(pieces, 1)
    spread = jnp.broadcast_to(payload[None], (devices,) + payload.shape)
    table = lax.all_to_all(spread, MESH_AXES, 0, 0)
    table = table.reshape(total_parents, payload.shape[1])

    near = near_field(counts, padded, cells)
    mine = (lax.axis_index(MESH_AXES) * per_device).astype(jnp.int32).reshape(1)
    downward = l2l.transpose(1, 0, 2)
    return translate(mine, counts, table, m2l, offsets, near, downward, lists, wide)


def solution(mesh):
    placed = (
        P(None, "gx", "gy", "gz", None),
        P("gx", "gy", "gz", None),
        P("gx", "gy", "gz"),
        P(("gx", "gy", "gz")),
        P(("gx", "gy", "gz"), None),
        P(("gx", "gy", "gz"), None),
        P(),
        P(),
        P(),
    )
    return jax.shard_map(
        per_block, mesh=mesh, in_specs=placed, out_specs=P("gx", "gy", "gz", None), check_vma=False
    )
```

time: 89.7 us -> 84.8 us (0.945)
  the two profiles are of different devices: /device:TPU:2 before, /device:TPU:14 now
where the time goes in v2:
time: 84.8 us; the launch traced here: 84 us
  Pallas kernels  47.6 us (56%)
  starting transfers between devices  17.9 us (21%)
  other arithmetic  9.19 us (11%)
  waiting for transfers between devices  6.61 us (8%)
  local copies, waits for them, and re-layouts  2.41 us (3%)
    pallas_call x1, Pallas kernels, near_field(): pl.pallas_call(functools.partial(near_body, cells), out_shape=jax.ShapeDt...  30.7 us
    pallas_call x1, Pallas kernels, translate(): pl.pallas_call(functools.partial(translate_body, (cells, per_device, list...  10.5 us
    pallas_call x1, Pallas kernels, multipole(): pl.pallas_call(functools.partial(multipole_body, cells), out_shape=jax.Sh...  6.47 us
    ppermute x2, starting transfers between devices, padded_along(): after = lax.ppermute(leading, axis, [(j, i) for i, j in up])  6.09 us
    all_to_all x1, starting transfers between devices, per_block(): table = lax.all_to_all(spread, MESH_AXES, 0, 0)  5.96 us
    ppermute x2, starting transfers between devices, padded_along(): before = lax.ppermute(last, axis, up)  5.32 us
    ppermute x2, waiting for transfers between devices, padded_along(): after = lax.ppermute(leading, axis, [(j, i) for i, j in up])  3.14 us
    ppermute x2, waiting for transfers between devices, padded_along(): before = lax.ppermute(last, axis, up)  2.94 us
  transfers between devices with their start and end apart: 6, of which 3 were waited for; matrix products, arithmetic and copies ran while one was open for 10% of the time, Pallas kernels for 44%

profile of v2, /device:TPU:14, one launch (start us, length us, event | category | flops | bytes accessed | tf_op | source)
XLA Modules:
  0.0 84.0 jit_solution(4698957962111789366)
XLA Ops:
  0.0 0.8 fusion.26
  0.8 1.0 %broadcast_select_fusion.2 = f32[4,2,4,1,256]{4,3,2,1,0:T(1,128)S(1)} fusion(pred[]{:T(512)S(6)} %eq.18, f32[1,2,4,4,256]{4,3,2,1,0:T(4,128)S(1)} %fusion.26, f32[3,2,4,4,256]{4,3,2,1,0:T(4,128)} %offsets.3), kind=kLoop, calls=%fused_computation.8 | loop fusion | flops 24576 | bytes 163841 | tf_op jit(solution)/shard_map/jit(_where)/select_n | solution.py:454
  1.9 0.6 collective-permute-start
  2.4 1.4 %fusion.charges = f32[2,4,4,256]{3,2,1,0:T(4,128)} fusion(f32[2,4,4,256]{3,2,1,0:T(4,128)} %param.12, s32[2,4,4]{2,1,0:T(4,128)} %counts.3), kind=kLoop, calls=%fused_computation.11 | loop fusion | flops 16384 | bytes 65664 | tf_op jit(solution)/shard_map/mul | solution.py:485
  3.9 0.7 fusion.12
  4.6 0.7 convert_bitcast_fusion
  5.3 0.5 collective-permute-done
  5.9 0.8 pad_maximum_fusion.5
  6.7 1.9 %collective-permute-start.1 = (f32[4,2,1,6,256]{4,3,2,1,0:T(8,128)S(1)}, f32[4,2,1,6,256]{4,3,2,1,0:T(8,128)S(1)}, u32[]{:S(2)}, u32[]{:S(2)}) collective-permute-start(f32[4,2,1,6,256]{4,3,2,1,0:T(8,128)S(1)} %get-tuple-element.9), channel_id=1, source_target_pairs={{0,2},{2,4},{4,6},{1,3},{3,5},{5,7},{8,10},{10,12},{12,14},{9,11},... | collective-permute-start | bytes 147464 | tf_op jit(solution)/shard_map/ppermute | solution.py:459
  8.6 3.6 %collective-permute-start.2 = (f32[4,2,1,6,256]{4,3,2,1,0:T(8,128)S(1)}, f32[4,2,1,6,256]{4,3,2,1,0:T(8,128)S(1)}, u32[]{:S(2)}, u32[]{:S(2)}) collective-permute-start(f32[4,2,1,6,256]{4,3,2,1,0:T(8,128)S(1)} %get-tuple-element.10), channel_id=1, source_target_pairs={{2,0},{4,2},{6,4},{3,1},{5,3},{7,5},{10,8},{12,10},{14,12},{11,9},... | collective-permute-start | bytes 147464 | tf_op jit(solution)/shard_map/ppermute | solution.py:460
  12.5 0.7 convert_element_type.28
  13.2 6.5 %multipole.1 = bf16[4,121]{1,0:T(4,128)(2,1)} custom-call(f32[3,2,4,4,256]{4,3,2,1,0:T(4,128)} %offsets.3, f32[2,4,4,256]{3,2,1,0:T(4,128)} %fusion.charges, f32[121,8,121]{2,1,0:T(8,128)} %bitcast.10), custom_call_target="tpu_custom_call" | custom-call | tf_op jit(solution)/shard_map/multipole/pallas_call | solution.py:313
  19.7 0.7 concatenate.15
  20.4 0.7 broadcast_in_dim.10
  21.2 6.0 %all-to-all-start = ((bf16[32,4,640]{2,1,0:T(4,128)(2,1)}), bf16[32,4,640]{2,1,0:T(4,128)(2,1)S(1)}, u32[]{:S(2)}, u32[]{:S(2)}) async-start(bf16[32,4,640]{2,1,0:T(4,128)(2,1)} %broadcast_in_dim.10), calls=%async_computation | async-start | bytes 327680 | tf_op jit(solution)/shard_map/all_to_all | solution.py:512
  27.1 1.0 %pad_maximum_fusion.1 = f32[4,2,6,6,256]{4,3,2,1,0:T(8,128)S(1)} fusion(f32[4,2,1,6,256]{4,3,2,1,0:T(8,128)S(1)} %collective-permute-done.2, f32[4,2,4,1,256]{4,3,2,1,0:T(1,128)S(1)} %get-tuple-element.12, f32[1,2,4,4,256]{4,3,2,1,0:T(4,128)S(1)} %fusion.26, f32[3,2,4,4,256]{4,3,2,1,0:T(4,128)} %offsets.3, f32[4,2,4,1,256]{4,3,2,1,0:T(1,128)S(1)} %get-tuple-element.11, ...), kind=kLoop, calls=%fused_computation.1 | loop fusion | flops 368640 | bytes 589824 | tf_op jit(solution)/shard_map/concatenate | solution.py:461
  28.2 3.4 %collective-permute-start.3 = (f32[4,1,6,6,256]{4,3,2,1,0:T(8,128)S(1)}, f32[4,1,6,6,256]{4,3,2,1,0:T(8,128)S(1)}, u32[]{:S(2)}, u32[]{:S(2)}) collective-permute-start(f32[4,1,6,6,256]{4,3,2,1,0:T(8,128)S(1)} %get-tuple-element.7), channel_id=1, source_target_pairs={{0,8},{8,16},{16,24},{1,9},{9,17},{17,25},{2,10},{10,18},{18,26},{... | collective-permute-start | bytes 442376 | tf_op jit(solution)/shard_map/ppermute | solution.py:459
  31.6 2.4 %collective-permute-start.4 = (f32[4,1,6,6,256]{4,3,2,1,0:T(8,128)S(1)}, f32[4,1,6,6,256]{4,3,2,1,0:T(8,128)S(1)}, u32[]{:S(2)}, u32[]{:S(2)}) collective-permute-start(f32[4,1,6,6,256]{4,3,2,1,0:T(8,128)S(1)} %get-tuple-element.8), channel_id=1, source_target_pairs={{8,0},{16,8},{24,16},{9,1},{17,9},{25,17},{10,2},{18,10},{26,18},{... | collective-permute-start | bytes 442376 | tf_op jit(solution)/shard_map/ppermute | solution.py:460
  34.1 2.9 %collective-permute-done.3 = f32[4,1,6,6,256]{4,3,2,1,0:T(8,128)S(1)} collective-permute-done((f32[4,1,6,6,256]{4,3,2,1,0:T(8,128)S(1)}, f32[4,1,6,6,256]{4,3,2,1,0:T(8,128)S(1)}, u32[]{:S(2)}, u32[]{:S(2)}) %collective-permute-start.3) | collective-permute-done | bytes 147488 | tf_op jit(solution)/shard_map/ppermute | solution.py:459
  37.0 3.1 %collective-permute-done.4 = f32[4,1,6,6,256]{4,3,2,1,0:T(8,128)S(1)} collective-permute-done((f32[4,1,6,6,256]{4,3,2,1,0:T(8,128)S(1)}, f32[4,1,6,6,256]{4,3,2,1,0:T(8,128)S(1)}, u32[]{:S(2)}, u32[]{:S(2)}) %collective-permute-start.4) | collective-permute-done | bytes 147488 | tf_op jit(solution)/shard_map/ppermute | solution.py:460
  40.1 1.9 %pad_maximum_fusion.source = f32[4,4,6,6,256]{4,3,2,1,0:T(8,128)} fusion(f32[4,1,6,6,256]{4,3,2,1,0:T(8,128)S(1)} %collective-permute-done.4, f32[4,2,1,6,256]{4,3,2,1,0:T(8,128)S(1)} %collective-permute-done.2, f32[4,2,4,1,256]{4,3,2,1,0:T(1,128)S(1)} %get-tuple-element.12, f32[1,2,4,4,256]{4,3,2,1,0:T(4,128)S(1)} %fusion.26, f32[3,2,4,4,256]{4,3,2,1,0:T(4,128)} %offsets.3, ...), kind=kLoop, calls=%fused_computation | loop fusion | flops 1032192 | bytes 1179648 | tf_op jit(solution)/shard_map/concatenate | solution.py:461
  42.0 30.7 %near.1 = f32[32,256]{1,0:T(8,128)} custom-call(s32[2,4,4]{2,1,0:T(4,128)} %counts.3, f32[4,4,6,6,256]{4,3,2,1,0:T(8,128)} %pad_maximum_fusion.source, bf16[27,32,128]{2,1,0:T(8,128)(2,1)} %constant.217.clone.table, bf16[16,128]{1,0:T(8,128)(2,1)} %constant.218.clone.expand), custom_call_target="tpu_custom_call" | custom-call | tf_op jit(solution)/shard_map/near/pallas_call | solution.py:183
  72.7 0.7 reshape.35.table
  73.4 10.5 %translate.1 = f32[2,4,4,256]{3,2,1,0:T(4,128)} custom-call(s32[1]{0:T(128)} %bitcast.mine, s32[2,4,4]{2,1,0:T(4,128)} %counts.3, bf16[128,640]{1,0:T(8,128)(2,1)} %reshape.35.table, bf16[121,121,256]{2,1,0:T(8,128)(2,1)} %remote.1, f32[3,2,4,4,256]{4,3,2,1,0:T(4,128)} %offsets.3, f32[32,256]{1,0:T(8,128)} %near.1, f32[121,8,121]{2,1,0:T(8,128)} %bitcast.9), custom_call_target="tpu_custom_call" | custom-call | tf_op jit(solution)/shard_map/translate/pallas_call | solution.py:421
  (11 shorter events, 0.3 us)
Async XLA Ops:
  1.9 4.0 %collective-permute-start = (f32[4,2,4,1,256]{4,3,2,1,0:T(1,128)S(1)}, f32[4,2,4,1,256]{4,3,2,1,0:T(1,128)S(1)}, u32[]{:S(2)}, u32[]{:S(2)}) collective-permute-start(f32[4,2,4,1,256]{4,3,2,1,0:T(1,128)S(1)} %broadcast_select_fusion.2), channel_id=1, source_target_pairs={{0,1},{1,0},{2,3},{3,2},{4,5},{5,4},{6,7},{7,6},{8,9},{9,8},{10,11... | collective-permute-start | bytes 98312 | tf_op jit(solution)/shard_map/ppermute | solution.py:454
  6.7 20.4 %collective-permute-start.1 = (f32[4,2,1,6,256]{4,3,2,1,0:T(8,128)S(1)}, f32[4,2,1,6,256]{4,3,2,1,0:T(8,128)S(1)}, u32[]{:S(2)}, u32[]{:S(2)}) collective-permute-start(f32[4,2,1,6,256]{4,3,2,1,0:T(8,128)S(1)} %get-tuple-element.9), channel_id=1, source_target_pairs={{0,2},{2,4},{4,6},{1,3},{3,5},{5,7},{8,10},{10,12},{12,14},{9,11},... | collective-permute-start | bytes 147464 | tf_op jit(solution)/shard_map/ppermute | solution.py:459
  8.6 18.5 %collective-permute-start.2 = (f32[4,2,1,6,256]{4,3,2,1,0:T(8,128)S(1)}, f32[4,2,1,6,256]{4,3,2,1,0:T(8,128)S(1)}, u32[]{:S(2)}, u32[]{:S(2)}) collective-permute-start(f32[4,2,1,6,256]{4,3,2,1,0:T(8,128)S(1)} %get-tuple-element.10), channel_id=1, source_target_pairs={{2,0},{4,2},{6,4},{3,1},{5,3},{7,5},{10,8},{12,10},{14,12},{11,9},... | collective-permute-start | bytes 147464 | tf_op jit(solution)/shard_map/ppermute | solution.py:460
  21.2 51.6 %all-to-all-start = ((bf16[32,4,640]{2,1,0:T(4,128)(2,1)}), bf16[32,4,640]{2,1,0:T(4,128)(2,1)S(1)}, u32[]{:S(2)}, u32[]{:S(2)}) async-start(bf16[32,4,640]{2,1,0:T(4,128)(2,1)} %broadcast_in_dim.10), calls=%async_computation | async-start | bytes 327680 | tf_op jit(solution)/shard_map/all_to_all | solution.py:512
  28.2 8.8 %collective-permute-start.3 = (f32[4,1,6,6,256]{4,3,2,1,0:T(8,128)S(1)}, f32[4,1,6,6,256]{4,3,2,1,0:T(8,128)S(1)}, u32[]{:S(2)}, u32[]{:S(2)}) collective-permute-start(f32[4,1,6,6,256]{4,3,2,1,0:T(8,128)S(1)} %get-tuple-element.7), channel_id=1, source_target_pairs={{0,8},{8,16},{16,24},{1,9},{9,17},{17,25},{2,10},{10,18},{18,26},{... | collective-permute-start | bytes 442376 | tf_op jit(solution)/shard_map/ppermute | solution.py:459
  31.6 8.5 %collective-permute-start.4 = (f32[4,1,6,6,256]{4,3,2,1,0:T(8,128)S(1)}, f32[4,1,6,6,256]{4,3,2,1,0:T(8,128)S(1)}, u32[]{:S(2)}, u32[]{:S(2)}) collective-permute-start(f32[4,1,6,6,256]{4,3,2,1,0:T(8,128)S(1)} %get-tuple-element.8), channel_id=1, source_target_pairs={{8,0},{16,8},{24,16},{9,1},{17,9},{25,17},{10,2},{18,10},{26,18},{... | collective-permute-start | bytes 442376 | tf_op jit(solution)/shard_map/ppermute | solution.py:460

commit v3 on v2

--- a/solution.py
+++ b/solution.py
@@ -15,37 +15,34 @@
 DEPTH = 80
 
 
-def delta_tables():
-    table = np.zeros((27, 32, 128), np.float32)
-    for index, delta in enumerate(DELTAS):
-        for axis in range(3):
-            for group in range(3):
-                table[index, 3 * group + axis] = 2.0 * delta[axis]
-                table[index, 16 + 3 * group + axis] = delta[axis]
-        rest = np.float32(sum(d * d for d in delta) + SOFTENING)
-        for part in range(3):
-            piece = np.asarray(rest).astype(jnp.bfloat16).astype(np.float32)
-            table[index, 25 + part] = piece
-            rest = np.float32(rest - piece)
-    return table
-
-
-def expand_table():
-    table = np.zeros((16, 128), np.float32)
+def delta_rows(delta):
+    row = iota((32, 128), 0)
+    values = jnp.zeros((32, 128), jnp.float32)
     for axis in range(3):
-        first, second, third = axis, 3 + axis, 6 + axis
-        for group in range(3):
-            table[first, 3 * group + axis] = -2.0
-            table[12, 48 + 3 * group + axis] = 1.0
-        for group in range(2):
-            table[second, 16 + 3 * group + axis] = -2.0
-        table[third, 32 + axis] = -2.0
-        table[12, 9 + axis] = 1.0
-        table[9 + axis, 12 + axis] = 1.0
-        for group, source in enumerate((first, second, third)):
-            table[source, 64 + 3 * group + axis] = -2.0
-        table[12, 73 + axis] = 1.0
-    return table
+        values = jnp.where((row < 9) & (row % 3 == axis), 2.0 * delta[axis], values)
+        values = jnp.where((row >= 16) & (row < 25) & (row % 3 == (axis + 1) % 3), delta[axis], values)
+    rest = np.float32(sum(d * d for d in delta) + SOFTENING)
+    for part in range(3):
+        piece = np.asarray(rest).astype(jnp.bfloat16).astype(np.float32)
+        values = jnp.where(row == 25 + part, float(piece), values)
+        rest = np.float32(rest - piece)
+    return values
+
+
+def expand_rows():
+    row, col = iota((32, 128), 0), iota((32, 128), 1)
+    slot = col % 16
+    triple, axis = slot // 3, slot % 3
+    field = col // 16
+    known = slot < 9
+    product = (field < 3) & known & (triple < 3 - field) & (row == 3 * field + axis)
+    offset = (field == 4) & known & (row == slot)
+    plain = (field == 0) & (slot >= 9) & (slot < 12) & (row == 12)
+    norm = (field == 0) & (slot >= 12) & (slot < 15) & (row == slot - 3)
+    shift = (field == 3) & known & (row == 12)
+    rest = (field == 4) & (slot >= 9) & (slot < 12) & (row == 12)
+    values = jnp.where(product | offset, -2.0, 0.0)
+    return jnp.where(plain | norm | shift | rest, 1.0, values)
 
 
 def split3(value):
@@ -72,15 +69,17 @@
     return lax.dot_general(narrow(left), narrow(right), dims, preferred_element_type=jnp.float32)
 
 
-def near_body(cells, counts, source, table, expand, out, rows32, base, left, total):
+def near_body(cells, counts, lower, middle, upper, out, rows32, base, left, total, table):
     cells_x, cells_y, cells_z = cells
-    _, pad_x, pad_y, pad_z, width = source.shape
+    _, _, pad_y, pad_z, width = middle.shape
+    pad_x = cells_x + 2
     leaves = cells_x * cells_y * cells_z
     tiles = width // 128
     sources = pad_x * pad_y * pad_z
 
-    def fill(column, carry):
-        a, b = column // pad_y, column % pad_y
+    def fill(source, first, place, carry):
+        a, b = place // pad_y, place % pad_y
+        column = first * pad_y + place
         parts, norm = [], 0.0
         for axis in range(3):
             centred = source[axis, a, b] - 0.5
@@ -100,7 +99,12 @@
             base[leaf, :, 128 * part : 128 * part + 128] = narrow(rows32[pl.ds(start, 16), :])
         return carry
 
-    lax.fori_loop(0, pad_x * pad_y, fill, 0)
+    for index, delta in enumerate(DELTAS):
+        table[index] = narrow(delta_rows(delta))
+    table[len(DELTAS)] = narrow(expand_rows())
+    for source, first in ((lower, 0), (middle, 1), (upper, cells_x + 1)):
+        columns = source.shape[1] * pad_y
+        lax.fori_loop(0, columns, functools.partial(fill, source, first), 0, unroll=2)
     lax.fori_loop(0, pad_x * pad_y * pad_z, pack, 0, unroll=8)
 
     def place(leaf):
@@ -116,7 +120,7 @@
 
     def fill_left(leaf):
         features = base[home(leaf)].astype(jnp.float32).T
-        left[leaf % 2] = narrow(multiply(features, expand[...]))
+        left[leaf % 2] = narrow(multiply(features, table[len(DELTAS), 0:16]))
 
     ones = jnp.ones((8, 128), jnp.bfloat16)
     across = (((1,), (1,)), ((), ()))
@@ -173,12 +177,10 @@
     finish(leaves - 1)
 
 
-def near_field(counts, padded, cells):
+def near_field(counts, slabs, cells):
     leaves = cells[0] * cells[1] * cells[2]
-    width = padded.shape[-1]
-    sources = padded.shape[1] * padded.shape[2] * padded.shape[3]
-    table = jnp.asarray(delta_tables(), jnp.bfloat16)
-    expand = jnp.asarray(expand_table(), jnp.bfloat16)
+    width = slabs[1].shape[-1]
+    sources = (cells[0] + 2) * slabs[1].shape[2] * slabs[1].shape[3]
     vmem = pl.BlockSpec(memory_space=pltpu.VMEM)
     return pl.pallas_call(
         functools.partial(near_body, cells),
@@ -190,9 +192,16 @@
             pltpu.VMEM((sources, 16, width), jnp.bfloat16),
             pltpu.VMEM((2, width, 128), jnp.bfloat16),
             pltpu.VMEM((2, width, 128), jnp.float32),
+            pltpu.VMEM((len(DELTAS) + 1, 32, 128), jnp.bfloat16),
         ],
+        cost_estimate=pl.CostEstimate(
+            flops=leaves * 27 * width * width * 2 * DEPTH,
+            transcendentals=leaves * 27 * width * width,
+            bytes_accessed=sources * 4 * width * 4,
+        ),
+        compiler_params=pltpu.CompilerParams(vmem_limit_bytes=24 << 20),
         name="near",
-    )(counts, padded, table, expand)
+    )(counts, *slabs)
 
 
 def emit_harmonics(coord_x, coord_y, coord_z, emit):
@@ -241,10 +250,23 @@
             flat[first : first + size_z, :] = field[a, b]
 
 
-def fill_basis(offsets, flat, basis):
+def flatten_children(field, flat, cells):
+    _, cells_y, cells_z = cells
+    for parent in range(flat.shape[0] // 8):
+        for octant in range(0, 8, 2):
+            leaf = child_leaf(parent, octant, cells)
+            a, b, c = leaf // (cells_y * cells_z), leaf // cells_z % cells_y, leaf % cells_z
+            first = 8 * parent + octant
+            flat[first : first + 2, :] = field[a, b, c : c + 2]
+
+
+def fill_basis(offsets, flat, basis, cells=None):
     leaves = flat.shape[1]
     for axis in range(3):
-        flatten(offsets.at[axis], flat.at[axis])
+        if cells:
+            flatten_children(offsets.at[axis], flat.at[axis], cells)
+        else:
+            flatten(offsets.at[axis], flat.at[axis])
     for first in range(0, leaves, 8):
         rows = slice(first, first + 8)
         x, y, z = (flat[axis, rows, :] - 0.5 for axis in range(3))
@@ -267,11 +289,47 @@
     return (x * cells_y + y) * cells_z + z
 
 
-def multipole_body(cells, offsets, charges, upward, out, flat, charge, basis, sums):
+def limits(counts, first, size, width):
+    _, size_y, size_z = counts.shape
+    rows = iota((size, width), 0)
+    limit = jnp.zeros((size, width), jnp.int32)
+    for row in range(size):
+        leaf = first + row
+        count = counts[leaf // (size_y * size_z), leaf // size_z % size_y, leaf % size_z]
+        limit = jnp.where(rows == row, count, limit)
+    return limit
+
+
+def over(value, divisor):
+    return jnp.floor((value + 0.5) * (1.0 / divisor))
+
+
+def columns(cell, halves, peers):
+    (half_x, half_y, half_z), (_, count_y, count_z) = halves, peers
+    parents_y, parents_z = half_y * count_y, half_z * count_z
+    cell_a = over(cell, parents_y * parents_z)
+    rest = cell - cell_a * (parents_y * parents_z)
+    cell_b = over(rest, parents_z)
+    cell_c = rest - cell_b * parents_z
+    device, local = 0.0, 0.0
+    for part, half, count in zip((cell_a, cell_b, cell_c), halves, peers):
+        owner = over(part, half)
+        device = device * count + owner
+        local = local * half + (part - owner * half)
+    return device * (half_x * half_y * half_z) + local
+
+
+def multipole_body(info, counts, owned, offsets, charges, upward, sources, classes, out, *scratch):
+    cells, peers, wide = info
+    flat, charge, basis, sums = scratch
     leaves, width = charge.shape
     coef = upward.shape[0]
     per_device = leaves // 8
+    halves = tuple(size // 2 for size in cells)
     flatten(charges, charge)
+    for first in range(0, leaves, 8):
+        live = iota((8, width), 1) < limits(counts, first, 8, width)
+        charge[first : first + 8, :] = jnp.where(live, charge[first : first + 8, :], 0.0)
     fill_basis(offsets, flat, basis)
     parts = jnp.concatenate(split3(charge[...]) + (jnp.zeros((128 - 3 * leaves, width)),), 0)
     columns_all = parts.T
@@ -297,23 +355,52 @@
     wanted = child_leaf(col // span, slot // 3, cells) + leaves * (slot % 3)
     chosen = multiply(stacked, mask((row == wanted) & (slot < 24)))
     slot = lane % span
-    result = jnp.zeros((coef, 128), jnp.float32)
-    for octant in range(8):
-        for j, left in enumerate(split3(upward[:, octant, :])):
-            right = jnp.where((slot >= 3 * octant) & (slot < 3 * octant + 3 - j), chosen, 0.0)
-            result = result + multiply(left, right)
-    out[...] = narrow(jnp.sum(result.T.reshape(per_device, span, coef), 1))
-
-
-def multipole(offsets, charge_live, upward):
-    cells, width = charge_live.shape[:3], charge_live.shape[3]
+    result = jnp.zeros((coef * 8, 128), jnp.float32)
+    for j, left in enumerate(split3(upward[...].reshape(coef * 8, coef))):
+        result = result + multiply(left, jnp.where(slot % 3 < 3 - j, chosen, 0.0))
+    shape = (coef, 8, 128)
+    result = jnp.where(iota(shape, 1) == iota(shape, 2) % span // 3, result.reshape(shape), 0.0)
+    parent = jnp.sum(jnp.sum(result, 1).T.reshape(per_device, span, coef), 1)
+
+    def wider(value, size):
+        fill = jnp.zeros((per_device, size - value.shape[1]), jnp.float32)
+        return jnp.concatenate([value, fill], 1)
+
+    shape = (per_device, 128)
+    cell = jnp.zeros(shape, jnp.float32)
+    for row in range(per_device):
+        cell = jnp.where(iota(shape, 0) == row, owned[row].astype(jnp.float32), cell)
+    column = columns(cell, halves, peers)
+    upper = over(column, 256)
+    head = wider(parent, 128)
+    head = jnp.where(iota(shape, 1) == coef, column - 256.0 * upper, head)
+    head = jnp.where(iota(shape, 1) == coef + 1, upper, head)
+    column = columns(sources[...].astype(jnp.float32), halves, peers)
+    upper = over(column, 256)
+    pieces = [head, wider(classes[...].astype(jnp.float32), 256)]
+    pieces.append(wider(column - 256.0 * upper, 256))
+    if wide == 3:
+        pieces.append(wider(upper, 256))
+    payload = narrow(jnp.concatenate(pieces, 1))
+
+    def spread(device, carry):
+        out[device] = payload
+        return carry
+
+    lax.fori_loop(0, out.shape[0], spread, 0, unroll=8)
+
+
+def multipole(counts, owned, offsets, charges, upward, sources, classes, peers, wide):
+    cells, width = charges.shape[:3], charges.shape[3]
     leaves = cells[0] * cells[1] * cells[2]
     coef = upward.shape[0]
+    devices = peers[0] * peers[1] * peers[2]
+    smem = pl.BlockSpec(memory_space=pltpu.SMEM)
     vmem = pl.BlockSpec(memory_space=pltpu.VMEM)
     return pl.pallas_call(
-        functools.partial(multipole_body, cells),
-        out_shape=jax.ShapeDtypeStruct((leaves // 8, coef), jnp.bfloat16),
-        in_specs=[vmem] * 3,
+        functools.partial(multipole_body, (cells, peers, wide)),
+        out_shape=jax.ShapeDtypeStruct((devices, leaves // 8, 128 + 256 * wide), jnp.bfloat16),
+        in_specs=[smem, smem] + [vmem] * 5,
         out_specs=vmem,
         scratch_shapes=[
             pltpu.VMEM((3, leaves, width), jnp.float32),
@@ -322,25 +409,40 @@
             pltpu.VMEM((coef, 128), jnp.float32),
         ],
         name="multipole",
-    )(offsets, charge_live, upward)
-
-
-def translate_body(info, mine, counts, table, remote, offsets, near, downward, out, *scratch):
+    )(counts, owned, offsets, charges, upward, sources, classes)
+
+
+FETCHES = 11
+
+
+def translate_body(info, mine, counts, arrived, remote, offsets, near, downward, out, *scratch):
     cells, per_device, lists, wide = info
-    matrix, weights, sums, flat, basis, spread_local, sem = scratch
-    fetch = pltpu.make_async_copy(remote, matrix, sem)
-    fetch.start()
+    table, matrix, weights, sums, flat, basis, spread_local, sem = scratch
     coef, _, ops = matrix.shape
-    leaves, width = near.shape
+    chunk = next(n for n in range(11, 0, -1) if coef % n == 0)
+    fetches = []
+    for start in range(0, coef, chunk):
+        window = pl.ds(start, chunk)
+        copy = pltpu.make_async_copy(remote.at[window], matrix.at[window], sem.at[start // chunk])
+        copy.start()
+        fetches.append(copy)
+    _, width = near.shape
     _, cells_y, cells_z = cells
     rows = table.shape[0]
     span = 128 // per_device
     blocks = -(-coef // span)
-    chunk = next(n for n in range(11, 0, -1) if coef % n == 0)
-    fill_basis(offsets, flat, basis)
+    fill_basis(offsets, flat, basis, cells)
+    group = 8 // per_device
+
+    def settle(index, carry):
+        rows = [arrived[index * group + part].astype(jnp.float32) for part in range(group)]
+        table[pl.ds(pl.multiple_of(8 * index, 8), 8), :] = jnp.concatenate(rows, 0)
+        return carry
+
+    lax.fori_loop(0, arrived.shape[0] // group, settle, 0, unroll=4)
 
     seg = 256
-    head = table[:, 0:128].astype(jnp.float32)
+    head = table[:, 0:128]
     owned = head[:, coef : coef + 1] + 256.0 * head[:, coef + 1 : coef + 2]
     lane = iota((rows, 128), 1)
     chosen = mask((owned.astype(jnp.int32) == lane + mine[0]) & (lane < per_device))
@@ -364,8 +466,10 @@
         tiled = multiply(parents, mask((row == span * block + col % span) & (row < coef)))
         stacked = [jnp.where(lane // span == row, tiled, 0.0) for row in range(per_device)]
         weights[block] = narrow(multiply(counted, jnp.concatenate(stacked, 0)))
-    fetch.wait()
     for start in range(0, coef, chunk):
+        if start // chunk % FETCHES == 0:
+            for copy in fetches[start // chunk : start // chunk + FETCHES]:
+                copy.wait()
         total = jnp.zeros((chunk, 128), jnp.float32)
         for block in range(blocks):
             height = min(span, coef - span * block)
@@ -380,34 +484,26 @@
         sums[start : start + chunk, :] = total
     gather = mask(iota((128, 128), 0) // span == iota((128, 128), 1))
     local = sum(multiply(piece, gather) for piece in split3(sums[...]))
-    local = jnp.concatenate(split3(local.T[0:8]), 0)
-    for octant in range(8):
-        result = jnp.zeros((8, coef), jnp.float32)
-        for j, right in enumerate(split3(downward[:, octant, :])):
-            product = multiply(local, right, across)
-            for i in range(3 - j):
-                result = result + product[8 * i : 8 * i + 8]
-        for parent in range(per_device):
+    parts = split3(local)
+    result = jnp.zeros((coef * 8, 128), jnp.float32)
+    for j, left in enumerate(split3(downward[...].reshape(coef * 8, coef))):
+        for right in parts[0 : 3 - j]:
+            result = result + multiply(left, right)
+    spread_local[...] = result
+    for parent in range(per_device):
+        rows = slice(8 * parent, 8 * parent + 8)
+        total = jnp.zeros((8, width), jnp.float32)
+        for index in range(coef):
+            values = spread_local[8 * index : 8 * index + 8, parent : parent + 1]
+            total = total + jnp.broadcast_to(values, (8, width)) * basis[index, rows, :]
+        for octant in range(0, 8, 2):
             leaf = child_leaf(parent, octant, cells)
-            spread_local[leaf : leaf + 1, 0:coef] = result[parent : parent + 1]
-    slot = iota((8, width), 1)
-    sub = iota((8, width), 0)
-    for first in range(0, leaves, 8):
-        values = spread_local[first : first + 8, :]
-        total = near[first : first + 8, :]
-        for index in range(coef):
-            column = jnp.broadcast_to(values[:, index : index + 1], (8, width))
-            total = total + column * basis[index, first : first + 8, :]
-        limit = jnp.zeros((8, width), jnp.int32)
-        for row in range(8):
-            leaf = first + row
-            count = counts[leaf // (cells_y * cells_z), leaf // cells_z % cells_y, leaf % cells_z]
-            limit = jnp.where(sub == row, count, limit)
-        total = jnp.where(slot < limit, total, 0.0)
-        for row in range(0, 8, cells_z):
-            leaf = first + row
-            a, b = leaf // (cells_y * cells_z), leaf // cells_z % cells_y
-            out[a, b] = total[row : row + cells_z]
+            a, b, c = leaf // (cells_y * cells_z), leaf // cells_z % cells_y, leaf % cells_z
+            limit = jnp.zeros((2, width), jnp.int32)
+            for row in range(2):
+                limit = jnp.where(iota((2, width), 0) == row, counts[a, b, c + row], limit)
+            value = total[octant : octant + 2] + near[leaf : leaf + 2, :]
+            out[a, b, c : c + 2, :] = jnp.where(iota((2, width), 1) < limit, value, 0.0)
 
 
 def translate(mine, counts, table, matrix, offsets, near, downward, lists, wide):
@@ -424,25 +520,20 @@
         in_specs=[smem, smem, vmem, pl.BlockSpec(memory_space=pl.ANY)] + [vmem] * 3,
         out_specs=vmem,
         scratch_shapes=[
+            pltpu.VMEM((table.shape[0] * table.shape[1], table.shape[2]), jnp.float32),
             pltpu.VMEM(matrix.shape, matrix.dtype),
             pltpu.VMEM((-(-coef // span), ops, 128), jnp.bfloat16),
             pltpu.VMEM((coef, 128), jnp.float32),
             pltpu.VMEM((3, leaves, width), jnp.float32),
             pltpu.VMEM((coef, leaves, width), jnp.float32),
-            pltpu.VMEM((leaves, 128), jnp.float32),
-            pltpu.SemaphoreType.DMA(()),
+            pltpu.VMEM((8 * coef, 128), jnp.float32),
+            pltpu.SemaphoreType.DMA((coef,)),
         ],
         name="translate",
     )(mine, counts, table, matrix, offsets, near, downward)
 
 
 MESH_AXES = ("gx", "gy", "gz")
-
-
-def extended(value, sides):
-    for axis, dim in sides:
-        value = padded_along(value, axis, dim)
-    return value
 
 
 def padded_along(value, axis, dim):
@@ -458,63 +549,32 @@
         up = [(i, i + 1) for i in range(peers - 1)]
         before = lax.ppermute(last, axis, up)
         after = lax.ppermute(leading, axis, [(j, i) for i, j in up])
-    return jnp.concatenate([before, value, after], axis=dim)
-
-
-def columns(cell, halves, peers):
-    (half_x, half_y, half_z), (_, count_y, count_z) = halves, peers
-    parents_y, parents_z = half_y * count_y, half_z * count_z
-    cell_a = cell // (parents_y * parents_z)
-    cell_b = cell // parents_z % parents_y
-    cell_c = cell % parents_z
-    device = (cell_a // half_x * count_y + cell_b // half_y) * count_z + cell_c // half_z
-    local = (cell_a % half_x * half_y + cell_b % half_y) * half_z + cell_c % half_z
-    return device * (half_x * half_y * half_z) + local
+    return before, value, after
 
 
 def per_block(offsets, charges, counts, owned_cell, list_sources, list_ops, m2m, m2l, l2l):
-    cells = cells_x, cells_y, cells_z = charges.shape[:3]
-    width = charges.shape[3]
-    halves = half_x, half_y, half_z = (cells_x // 2, cells_y // 2, cells_z // 2)
-    per_device = half_x * half_y * half_z
+    cells = charges.shape[:3]
+    per_device = cells[0] * cells[1] * cells[2] // 8
     peers = tuple(lax.axis_size(axis) for axis in MESH_AXES)
-    devices = peers[0] * peers[1] * peers[2]
-    total_parents = per_device * devices
-    slot_ids = jnp.arange(width, dtype=jnp.int32)
-    live = (slot_ids[None, None, None, :] < counts[..., None]).astype(jnp.float32)
-    charge_live = charges * live
-    stacked = jnp.concatenate([offsets, charge_live[None]], 0)
-    padded = extended(stacked, (("gz", 3), ("gy", 2), ("gx", 1)))
-
-    coef = m2m.shape[1]
-    parent_rows = multipole(offsets, charge_live, m2m.transpose(1, 0, 2))
-
-    lists = list_sources.shape[1]
+    total_parents = per_device * peers[0] * peers[1] * peers[2]
+    slot_ids = jnp.arange(charges.shape[3], dtype=jnp.int32)
+    charge_live = jnp.where(slot_ids[None, None, None, :] < counts[..., None], charges, 0.0)
+    padded = jnp.concatenate([offsets, charge_live[None]], 0)
+    for axis, dim in (("gz", 3), ("gy", 2)):
+        padded = jnp.concatenate(padded_along(padded, axis, dim), dim)
+    slabs = padded_along(padded, "gx", 1)
+
     wide = 2 if total_parents <= 256 else 3
-    owner_columns = columns(owned_cell, halves, peers)[:, None]
-    source_columns = columns(list_sources, halves, peers)
-
-    def segment(values, size):
-        values = values.astype(jnp.bfloat16)
-        return jnp.pad(values, ((0, 0), (0, size - values.shape[1])))
-
-    pieces = [
-        parent_rows,
-        segment(owner_columns % 256, 1),
-        segment(owner_columns // 256, 127 - coef),
-        segment(list_ops, 256),
-        segment(source_columns % 256, 256),
-    ]
-    if wide == 3:
-        pieces.append(segment(source_columns // 256, 256))
-    payload = jnp.concatenate(pieces, 1)
-    spread = jnp.broadcast_to(payload[None], (devices,) + payload.shape)
+    upward = m2m.transpose(1, 0, 2)
+    spread = multipole(
+        counts, owned_cell, offsets, charges, upward, list_sources, list_ops, peers, wide
+    )
     table = lax.all_to_all(spread, MESH_AXES, 0, 0)
-    table = table.reshape(total_parents, payload.shape[1])
-
-    near = near_field(counts, padded, cells)
+
+    near = near_field(counts, slabs, cells)
     mine = (lax.axis_index(MESH_AXES) * per_device).astype(jnp.int32).reshape(1)
     downward = l2l.transpose(1, 0, 2)
+    lists = list_sources.shape[1]
     return translate(mine, counts, table, m2l, offsets, near, downward, lists, wide)
 
 

time: 84.8 us -> 75.3 us (0.89)
  the two profiles are of different devices: /device:TPU:14 before, /device:TPU:31 now
where the time goes in v3:
time: 75.3 us; the launch traced here: 74.7 us
  Pallas kernels  45.3 us (60%)
  starting transfers between devices  20 us (27%)
  other arithmetic  3.71 us (5%)
  waiting for transfers between devices  3.42 us (5%)
  local copies, waits for them, and re-layouts  2.02 us (3%)
    pallas_call x1, Pallas kernels, near_field(): pl.pallas_call(functools.partial(near_body, cells), out_shape=jax.ShapeDt...  30.2 us
    pallas_call x1, Pallas kernels, translate(): pl.pallas_call(functools.partial(translate_body, (cells, per_device, list...  9.97 us
    all_to_all x1, starting transfers between devices, per_block(): table = lax.all_to_all(spread, MESH_AXES, 0, 0)  8.76 us
    ppermute x2, starting transfers between devices, padded_along(): after = lax.ppermute(leading, axis, [(j, i) for i, j in up])  8.36 us
    pallas_call x1, Pallas kernels, multipole(): pl.pallas_call(functools.partial(multipole_body, (cells, peers, wide)), o...  5.14 us
    ppermute x2, starting transfers between devices, padded_along(): before = lax.ppermute(last, axis, up)  2.58 us
    ppermute x1, waiting for transfers between devices, padded_along(): lax.ppermute(jnp.where(upper, leading, last), axis, [(0, 1), (1, 0)])  2.54 us
    unnamed x6, local copies, waits for them, and re-layouts  1.99 us
  transfers between devices with their start and end apart: 6, of which 2 were waited for; matrix products, arithmetic and copies ran while one was open for 0% of the time, Pallas kernels for 47%

profile of v3, /device:TPU:31, one launch (start us, length us, event | category | flops | bytes accessed | tf_op | source)
XLA Modules:
  0.0 74.7 jit_solution(14553583645637112262)
XLA Ops:
  0.0 0.8 %select_bitcast_fusion = f32[1,2,4,4,256]{4,3,2,1,0:T(4,128)S(1)} fusion(f32[2,4,4,256]{3,2,1,0:T(4,128)} %charges.1, s32[2,4,4]{2,1,0:T(4,128)} %counts.5), kind=kLoop, calls=%fused_computation.9 | loop fusion | flops 16384 | bytes 65664 | tf_op jit(solution)/shard_map/broadcast_in_dim | solution.py:562
  0.8 1.0 %broadcast_select_fusion.2 = f32[4,2,4,1,256]{4,3,2,1,0:T(1,128)S(1)} fusion(pred[]{:T(512)S(6)} %eq.3, f32[1,2,4,4,256]{4,3,2,1,0:T(4,128)S(1)} %select_bitcast_fusion, f32[3,2,4,4,256]{4,3,2,1,0:T(4,128)} %offsets.3), kind=kLoop, calls=%fused_computation.7 | loop fusion | flops 24576 | bytes 163841 | tf_op jit(solution)/shard_map/jit(_where)/select_n | solution.py:545
  1.9 0.3 collective-permute-start
  2.2 2.5 %collective-permute-done = f32[4,2,4,1,256]{4,3,2,1,0:T(1,128)S(1)} collective-permute-done((f32[4,2,4,1,256]{4,3,2,1,0:T(1,128)S(1)}, f32[4,2,4,1,256]{4,3,2,1,0:T(1,128)S(1)}, u32[]{:S(2)}, u32[]{:S(2)}) %collective-permute-start) | collective-permute-done | bytes 32800 | tf_op jit(solution)/shard_map/ppermute | solution.py:545
  4.8 0.8 %pad_maximum_fusion.4 = (f32[4,2,1,6,256]{4,3,2,1,0:T(8,128)S(1)}, f32[4,2,1,6,256]{4,3,2,1,0:T(8,128)S(1)}) fusion(f32[4,2,4,1,256]{4,3,2,1,0:T(1,128)S(1)} %get-tuple-element.10, f32[4,2,4,1,256]{4,3,2,1,0:T(1,128)S(1)} %get-tuple-element.9, f32[1,2,4,4,256]{4,3,2,1,0:T(4,128)S(1)} %select_bitcast_fusion, f32[3,2,4,4,256]{4,3,2,1,0:T(4,128)} %offsets.3), kind=kLoop, calls=%fused_computation.4 | loop fusion | flops 73728 | bytes 294912 | tf_op jit(solution)/shard_map/slice | solution.py:541
  5.6 1.3 %collective-permute-start.1 = (f32[4,2,1,6,256]{4,3,2,1,0:T(8,128)S(1)}, f32[4,2,1,6,256]{4,3,2,1,0:T(8,128)S(1)}, u32[]{:S(2)}, u32[]{:S(2)}) collective-permute-start(f32[4,2,1,6,256]{4,3,2,1,0:T(8,128)S(1)} %get-tuple-element.7), channel_id=1, source_target_pairs={{0,2},{2,4},{4,6},{1,3},{3,5},{5,7},{8,10},{10,12},{12,14},{9,11},... | collective-permute-start | bytes 147464 | tf_op jit(solution)/shard_map/ppermute | solution.py:550
  6.9 4.4 %collective-permute-start.2 = (f32[4,2,1,6,256]{4,3,2,1,0:T(8,128)S(1)}, f32[4,2,1,6,256]{4,3,2,1,0:T(8,128)S(1)}, u32[]{:S(2)}, u32[]{:S(2)}) collective-permute-start(f32[4,2,1,6,256]{4,3,2,1,0:T(8,128)S(1)} %get-tuple-element.8), channel_id=1, source_target_pairs={{2,0},{4,2},{6,4},{3,1},{5,3},{7,5},{10,8},{12,10},{14,12},{11,9},... | collective-permute-start | bytes 147464 | tf_op jit(solution)/shard_map/ppermute | solution.py:551
  11.2 0.0 collective-permute-done.1
  11.2 0.9 %collective-permute-done.2 = f32[4,2,1,6,256]{4,3,2,1,0:T(8,128)S(1)} collective-permute-done((f32[4,2,1,6,256]{4,3,2,1,0:T(8,128)S(1)}, f32[4,2,1,6,256]{4,3,2,1,0:T(8,128)S(1)}, u32[]{:S(2)}, u32[]{:S(2)}) %collective-permute-start.2) | collective-permute-done | bytes 49184 | tf_op jit(solution)/shard_map/ppermute | solution.py:551
  12.1 1.0 %pad_maximum_fusion.middle = f32[4,2,6,6,256]{4,3,2,1,0:T(8,128)S(1)} fusion(f32[4,2,1,6,256]{4,3,2,1,0:T(8,128)S(1)} %collective-permute-done.2, f32[4,2,4,1,256]{4,3,2,1,0:T(1,128)S(1)} %get-tuple-element.10, f32[1,2,4,4,256]{4,3,2,1,0:T(4,128)S(1)} %select_bitcast_fusion, f32[3,2,4,4,256]{4,3,2,1,0:T(4,128)} %offsets.3, ...), kind=kLoop, calls=%fused_computation | loop fusion | flops 368640 | bytes 589824 | tf_op jit(solution)/shard_map/concatenate | solution.py:564
  13.1 1.3 %collective-permute-start.3 = (f32[4,1,6,6,256]{4,3,2,1,0:T(8,128)S(1)}, f32[4,1,6,6,256]{4,3,2,1,0:T(8,128)S(1)}, u32[]{:S(2)}, u32[]{:S(2)}) collective-permute-start(f32[4,1,6,6,256]{4,3,2,1,0:T(8,128)S(1)} %get-tuple-element.6), channel_id=1, source_target_pairs={{0,8},{8,16},{16,24},{1,9},{9,17},{17,25},{2,10},{10,18},{18,26},{... | collective-permute-start | bytes 442376 | tf_op jit(solution)/shard_map/ppermute | solution.py:550
  14.4 4.0 %collective-permute-start.4 = (f32[4,1,6,6,256]{4,3,2,1,0:T(8,128)S(1)}, f32[4,1,6,6,256]{4,3,2,1,0:T(8,128)S(1)}, u32[]{:S(2)}, u32[]{:S(2)}) collective-permute-start(f32[4,1,6,6,256]{4,3,2,1,0:T(8,128)S(1)} %get-tuple-element.5), channel_id=1, source_target_pairs={{8,0},{16,8},{24,16},{9,1},{17,9},{25,17},{10,2},{18,10},{26,18},{... | collective-permute-start | bytes 442376 | tf_op jit(solution)/shard_map/ppermute | solution.py:551
  18.4 5.1 %multipole.1 = bf16[32,4,640]{2,1,0:T(4,128)(2,1)} custom-call(s32[2,4,4]{2,1,0:T(4,128)} %counts.5, s32[4]{0:T(128)} %owned.1, f32[3,2,4,4,256]{4,3,2,1,0:T(4,128)} %offsets.3, f32[2,4,4,256]{3,2,1,0:T(4,128)} %charges.1, f32[121,8,121]{2,1,0:T(8,128)} %bitcast.6, s32[4,189]{1,0:T(4,128)} %sources.1, s32[4,189]{1,0:T(4,128)} %classes.1), custom_call_target="tpu_custom_call" | custom-call | tf_op jit(solution)/shard_map/multipole/pallas_call | solution.py:400
  23.6 8.8 %all-to-all-start = ((bf16[32,4,640]{2,1,0:T(4,128)(2,1)}), bf16[32,4,640]{2,1,0:T(4,128)(2,1)S(1)}, u32[]{:S(2)}, u32[]{:S(2)}) async-start(bf16[32,4,640]{2,1,0:T(4,128)(2,1)} %multipole.1), calls=%async_computation | async-start | bytes 327680 | tf_op jit(solution)/shard_map/all_to_all | solution.py:572
  32.4 0.0 collective-permute-done.3.lower
  32.4 0.0 collective-permute-done.4.upper
  32.4 0.0 copy-start
  32.4 0.7 copy-done
  33.1 30.2 %near.1 = f32[32,256]{1,0:T(8,128)S(1)} custom-call(s32[2,4,4]{2,1,0:T(4,128)S(1)} %copy-done, f32[4,1,6,6,256]{4,3,2,1,0:T(8,128)S(1)} %collective-permute-done.3.lower, f32[4,2,6,6,256]{4,3,2,1,0:T(8,128)S(1)} %pad_maximum_fusion.middle, f32[4,1,6,6,256]{4,3,2,1,0:T(8,128)S(1)} %collective-permute-done.4.upper), custom_call_target="tpu_custom_call" | custom-call | flops 9059696640 | bytes 589824 | tf_op jit(solution)/shard_map/near/pallas_call | solution.py:185
  63.3 0.0 copy-start.1
  63.3 0.6 copy-done.1
  63.9 0.0 all-to-all-done.arrived
  63.9 0.7 copy-done.2
  64.6 10.0 %translate.1 = f32[2,4,4,256]{3,2,1,0:T(4,128)} custom-call(s32[1]{0:T(128)} %bitcast.mine, s32[2,4,4]{2,1,0:T(4,128)} %counts.5, bf16[32,4,640]{2,1,0:T(4,128)(2,1)} %copy-done.2, bf16[121,121,256]{2,1,0:T(8,128)(2,1)} %remote.1, f32[3,2,4,4,256]{4,3,2,1,0:T(4,128)} %offsets.3, f32[32,256]{1,0:T(8,128)} %copy-done.1, f32[121,8,121]{2,1,0:T(8,128)} %bitcast.5), custom_call_target="tpu_custom_call" | custom-call | tf_op jit(solution)/shard_map/translate/pallas_call | solution.py:517
  (3 shorter events, 0.1 us)
Async XLA Ops:
  1.9 2.8 %collective-permute-start = (f32[4,2,4,1,256]{4,3,2,1,0:T(1,128)S(1)}, f32[4,2,4,1,256]{4,3,2,1,0:T(1,128)S(1)}, u32[]{:S(2)}, u32[]{:S(2)}) collective-permute-start(f32[4,2,4,1,256]{4,3,2,1,0:T(1,128)S(1)} %broadcast_select_fusion.2), channel_id=1, source_target_pairs={{0,1},{1,0},{2,3},{3,2},{4,5},{5,4},{6,7},{7,6},{8,9},{9,8},{10,11... | collective-permute-start | bytes 98312 | tf_op jit(solution)/shard_map/ppermute | solution.py:545
  5.6 5.7 %collective-permute-start.1 = (f32[4,2,1,6,256]{4,3,2,1,0:T(8,128)S(1)}, f32[4,2,1,6,256]{4,3,2,1,0:T(8,128)S(1)}, u32[]{:S(2)}, u32[]{:S(2)}) collective-permute-start(f32[4,2,1,6,256]{4,3,2,1,0:T(8,128)S(1)} %get-tuple-element.7), channel_id=1, source_target_pairs={{0,2},{2,4},{4,6},{1,3},{3,5},{5,7},{8,10},{10,12},{12,14},{9,11},... | collective-permute-start | bytes 147464 | tf_op jit(solution)/shard_map/ppermute | solution.py:550
  6.9 5.2 %collective-permute-start.2 = (f32[4,2,1,6,256]{4,3,2,1,0:T(8,128)S(1)}, f32[4,2,1,6,256]{4,3,2,1,0:T(8,128)S(1)}, u32[]{:S(2)}, u32[]{:S(2)}) collective-permute-start(f32[4,2,1,6,256]{4,3,2,1,0:T(8,128)S(1)} %get-tuple-element.8), channel_id=1, source_target_pairs={{2,0},{4,2},{6,4},{3,1},{5,3},{7,5},{10,8},{12,10},{14,12},{11,9},... | collective-permute-start | bytes 147464 | tf_op jit(solution)/shard_map/ppermute | solution.py:551
  13.1 19.2 %collective-permute-start.3 = (f32[4,1,6,6,256]{4,3,2,1,0:T(8,128)S(1)}, f32[4,1,6,6,256]{4,3,2,1,0:T(8,128)S(1)}, u32[]{:S(2)}, u32[]{:S(2)}) collective-permute-start(f32[4,1,6,6,256]{4,3,2,1,0:T(8,128)S(1)} %get-tuple-element.6), channel_id=1, source_target_pairs={{0,8},{8,16},{16,24},{1,9},{9,17},{17,25},{2,10},{10,18},{18,26},{... | collective-permute-start | bytes 442376 | tf_op jit(solution)/shard_map/ppermute | solution.py:550
  14.4 17.9 %collective-permute-start.4 = (f32[4,1,6,6,256]{4,3,2,1,0:T(8,128)S(1)}, f32[4,1,6,6,256]{4,3,2,1,0:T(8,128)S(1)}, u32[]{:S(2)}, u32[]{:S(2)}) collective-permute-start(f32[4,1,6,6,256]{4,3,2,1,0:T(8,128)S(1)} %get-tuple-element.5), channel_id=1, source_target_pairs={{8,0},{16,8},{24,16},{9,1},{17,9},{25,17},{10,2},{18,10},{26,18},{... | collective-permute-start | bytes 442376 | tf_op jit(solution)/shard_map/ppermute | solution.py:551
  23.6 40.4 %all-to-all-start = ((bf16[32,4,640]{2,1,0:T(4,128)(2,1)}), bf16[32,4,640]{2,1,0:T(4,128)(2,1)S(1)}, u32[]{:S(2)}, u32[]{:S(2)}) async-start(bf16[32,4,640]{2,1,0:T(4,128)(2,1)} %multipole.1), calls=%async_computation | async-start | bytes 327680 | tf_op jit(solution)/shard_map/all_to_all | solution.py:572
  32.4 0.7 copy-start
  63.3 0.7 copy-start.1
  63.9 0.7 copy-start.2

commit v4 on v3

--- a/solution.py
+++ b/solution.py
@@ -104,8 +104,8 @@
     table[len(DELTAS)] = narrow(expand_rows())
     for source, first in ((lower, 0), (middle, 1), (upper, cells_x + 1)):
         columns = source.shape[1] * pad_y
-        lax.fori_loop(0, columns, functools.partial(fill, source, first), 0, unroll=2)
-    lax.fori_loop(0, pad_x * pad_y * pad_z, pack, 0, unroll=8)
+        lax.fori_loop(0, columns, functools.partial(fill, source, first), 0, unroll=6)
+    lax.fori_loop(0, pad_x * pad_y * pad_z, pack, 0, unroll=18)
 
     def place(leaf):
         return leaf // (cells_y * cells_z), leaf // cells_z % cells_y, leaf % cells_z
@@ -260,21 +260,22 @@
             flat[first : first + 2, :] = field[a, b, c : c + 2]
 
 
-def fill_basis(offsets, flat, basis, cells=None):
+def fill_basis(offsets, flat, basis):
     leaves = flat.shape[1]
     for axis in range(3):
-        if cells:
-            flatten_children(offsets.at[axis], flat.at[axis], cells)
-        else:
-            flatten(offsets.at[axis], flat.at[axis])
+        flatten(offsets.at[axis], flat.at[axis])
     for first in range(0, leaves, 8):
-        rows = slice(first, first + 8)
-        x, y, z = (flat[axis, rows, :] - 0.5 for axis in range(3))
-
-        def emit(index, value):
-            basis[index, rows, :] = value
-
-        emit_harmonics(x, y, z, emit)
+        fill_rows(flat, basis, first)
+
+
+def fill_rows(flat, basis, first):
+    rows = slice(first, first + 8)
+    x, y, z = (flat[axis, rows, :] - 0.5 for axis in range(3))
+
+    def emit(index, value):
+        basis[index, rows, :] = value
+
+    emit_harmonics(x, y, z, emit)
 
 
 def child_leaf(parent, octant, cells):
@@ -412,7 +413,7 @@
     )(counts, owned, offsets, charges, upward, sources, classes)
 
 
-FETCHES = 11
+FETCHES = 4
 
 
 def translate_body(info, mine, counts, arrived, remote, offsets, near, downward, out, *scratch):
@@ -426,12 +427,13 @@
         copy = pltpu.make_async_copy(remote.at[window], matrix.at[window], sem.at[start // chunk])
         copy.start()
         fetches.append(copy)
-    _, width = near.shape
+    leaves, width = near.shape
     _, cells_y, cells_z = cells
     rows = table.shape[0]
     span = 128 // per_device
     blocks = -(-coef // span)
-    fill_basis(offsets, flat, basis, cells)
+    for axis in range(3):
+        flatten_children(offsets.at[axis], flat.at[axis], cells)
     group = 8 // per_device
 
     def settle(index, carry):
@@ -454,18 +456,22 @@
     classes = entries[:, 0:seg].astype(jnp.int32)
     across = (((1,), (1,)), ((), ()))
     counted = []
+    fill_rows(flat, basis, 0)
     for row in range(per_device):
         from_cell = mask(iota((rows, seg), 0) == sources[row : row + 1])
         to_class = iota((ops, seg), 0) == classes[row : row + 1]
         to_class = mask(to_class & (iota((ops, seg), 1) < lists))
         counted.append(narrow(multiply(to_class, from_cell, across)))
     counted = jnp.concatenate(counted, 1)
+    for first in range(8, leaves - 8, 8):
+        fill_rows(flat, basis, first)
     parents = table[:, 0:128]
     for block in range(blocks):
         row, col = iota((128, 128), 0), iota((128, 128), 1)
         tiled = multiply(parents, mask((row == span * block + col % span) & (row < coef)))
         stacked = [jnp.where(lane // span == row, tiled, 0.0) for row in range(per_device)]
         weights[block] = narrow(multiply(counted, jnp.concatenate(stacked, 0)))
+    fill_rows(flat, basis, leaves - 8)
     for start in range(0, coef, chunk):
         if start // chunk % FETCHES == 0:
             for copy in fetches[start // chunk : start // chunk + FETCHES]:
@@ -484,12 +490,12 @@
         sums[start : start + chunk, :] = total
     gather = mask(iota((128, 128), 0) // span == iota((128, 128), 1))
     local = sum(multiply(piece, gather) for piece in split3(sums[...]))
-    parts = split3(local)
-    result = jnp.zeros((coef * 8, 128), jnp.float32)
-    for j, left in enumerate(split3(downward[...].reshape(coef * 8, coef))):
-        for right in parts[0 : 3 - j]:
-            result = result + multiply(left, right)
-    spread_local[...] = result
+    first, second, _ = split3(local)
+    for start in range(0, coef, chunk):
+        rows = downward[start : start + chunk].reshape(chunk * 8, coef)
+        upper, lower, _ = split3(rows)
+        result = multiply(upper, first) + (multiply(upper, second) + multiply(lower, first))
+        spread_local[8 * start : 8 * (start + chunk), :] = result
     for parent in range(per_device):
         rows = slice(8 * parent, 8 * parent + 8)
         total = jnp.zeros((8, width), jnp.float32)
@@ -529,6 +535,7 @@
             pltpu.VMEM((8 * coef, 128), jnp.float32),
             pltpu.SemaphoreType.DMA((coef,)),
         ],
+        compiler_params=pltpu.CompilerParams(vmem_limit_bytes=50 << 20),
         name="translate",
     )(mine, counts, table, matrix, offsets, near, downward)
 
@@ -557,6 +564,7 @@
     per_device = cells[0] * cells[1] * cells[2] // 8
     peers = tuple(lax.axis_size(axis) for axis in MESH_AXES)
     total_parents = per_device * peers[0] * peers[1] * peers[2]
+    sizes = jnp.minimum(counts, charges.shape[3])
     slot_ids = jnp.arange(charges.shape[3], dtype=jnp.int32)
     charge_live = jnp.where(slot_ids[None, None, None, :] < counts[..., None], charges, 0.0)
     padded = jnp.concatenate([offsets, charge_live[None]], 0)
@@ -571,11 +579,11 @@
     )
     table = lax.all_to_all(spread, MESH_AXES, 0, 0)
 
-    near = near_field(counts, slabs, cells)
+    near = near_field(sizes, slabs, cells)
     mine = (lax.axis_index(MESH_AXES) * per_device).astype(jnp.int32).reshape(1)
     downward = l2l.transpose(1, 0, 2)
     lists = list_sources.shape[1]
-    return translate(mine, counts, table, m2l, offsets, near, downward, lists, wide)
+    return translate(mine, sizes, table, m2l, offsets, near, downward, lists, wide)
 
 
 def solution(mesh):

time: 75.3 us -> 74.1 us (0.984)
  the two profiles are of different devices: /device:TPU:31 before, /device:TPU:14 now
where the time goes in v4:
time: 74.1 us; the launch traced here: 73.6 us
  Pallas kernels  42.1 us (57%)
  starting transfers between devices  18.1 us (24%)
  waiting for transfers between devices  8.65 us (12%)
  other arithmetic  4.4 us (6%)
    pallas_call x1, Pallas kernels, near_field(): pl.pallas_call(functools.partial(near_body, cells), out_shape=jax.ShapeDt...  29 us
    pallas_call x1, Pallas kernels, translate(): pl.pallas_call(functools.partial(translate_body, (cells, per_device, list...  7.97 us
    ppermute x2, starting transfers between devices, padded_along(): after = lax.ppermute(leading, axis, [(j, i) for i, j in up])  6.27 us
    all_to_all x1, starting transfers between devices, per_block(): table = lax.all_to_all(spread, MESH_AXES, 0, 0)  5.96 us
    ppermute x2, starting transfers between devices, padded_along(): before = lax.ppermute(last, axis, up)  5.32 us
    pallas_call x1, Pallas kernels, multipole(): pl.pallas_call(functools.partial(multipole_body, (cells, peers, wide)), o...  5.13 us
    ppermute x1, waiting for transfers between devices, padded_along(): lax.ppermute(jnp.where(upper, leading, last), axis, [(0, 1), (1, 0)])  3.41 us
    ppermute x2, waiting for transfers between devices, padded_along(): after = lax.ppermute(leading, axis, [(j, i) for i, j in up])  3.14 us
  transfers between devices with their start and end apart: 6, of which 3 were waited for; matrix products, arithmetic and copies ran while one was open for 2% of the time, Pallas kernels for 46%

profile of v4, /device:TPU:14, one launch (start us, length us, event | category | flops | bytes accessed | tf_op | source)
XLA Modules:
  0.0 73.6 jit_solution(9955272275931063241)
XLA Ops:
  0.0 0.8 %select_bitcast_fusion = f32[1,2,4,4,256]{4,3,2,1,0:T(4,128)S(1)} fusion(f32[2,4,4,256]{3,2,1,0:T(4,128)} %charges.1, s32[2,4,4]{2,1,0:T(4,128)} %counts.1), kind=kLoop, calls=%fused_computation.9 | loop fusion | flops 16384 | bytes 65664 | tf_op jit(solution)/shard_map/broadcast_in_dim | solution.py:570
  0.8 1.0 %broadcast_select_fusion.2 = f32[4,2,4,1,256]{4,3,2,1,0:T(1,128)S(1)} fusion(pred[]{:T(512)S(6)} %eq.3, f32[1,2,4,4,256]{4,3,2,1,0:T(4,128)S(1)} %select_bitcast_fusion, f32[3,2,4,4,256]{4,3,2,1,0:T(4,128)} %offsets.3), kind=kLoop, calls=%fused_computation.7 | loop fusion | flops 24576 | bytes 163841 | tf_op jit(solution)/shard_map/jit(_where)/select_n | solution.py:552
  1.9 0.6 collective-permute-start
  2.4 3.4 %collective-permute-done = f32[4,2,4,1,256]{4,3,2,1,0:T(1,128)S(1)} collective-permute-done((f32[4,2,4,1,256]{4,3,2,1,0:T(1,128)S(1)}, f32[4,2,4,1,256]{4,3,2,1,0:T(1,128)S(1)}, u32[]{:S(2)}, u32[]{:S(2)}) %collective-permute-start) | collective-permute-done | bytes 32800 | tf_op jit(solution)/shard_map/ppermute | solution.py:552
  5.9 0.8 %pad_maximum_fusion.4 = (f32[4,2,1,6,256]{4,3,2,1,0:T(8,128)S(1)}, f32[4,2,1,6,256]{4,3,2,1,0:T(8,128)S(1)}) fusion(f32[4,2,4,1,256]{4,3,2,1,0:T(1,128)S(1)} %get-tuple-element.10, f32[4,2,4,1,256]{4,3,2,1,0:T(1,128)S(1)} %get-tuple-element.9, f32[1,2,4,4,256]{4,3,2,1,0:T(4,128)S(1)} %select_bitcast_fusion, f32[3,2,4,4,256]{4,3,2,1,0:T(4,128)} %offsets.3), kind=kLoop, calls=%fused_computation.4 | loop fusion | flops 73728 | bytes 294912 | tf_op jit(solution)/shard_map/slice | solution.py:548
  6.7 1.9 %collective-permute-start.1 = (f32[4,2,1,6,256]{4,3,2,1,0:T(8,128)S(1)}, f32[4,2,1,6,256]{4,3,2,1,0:T(8,128)S(1)}, u32[]{:S(2)}, u32[]{:S(2)}) collective-permute-start(f32[4,2,1,6,256]{4,3,2,1,0:T(8,128)S(1)} %get-tuple-element.7), channel_id=1, source_target_pairs={{0,2},{2,4},{4,6},{1,3},{3,5},{5,7},{8,10},{10,12},{12,14},{9,11},... | collective-permute-start | bytes 147464 | tf_op jit(solution)/shard_map/ppermute | solution.py:557
  8.6 3.6 %collective-permute-start.2 = (f32[4,2,1,6,256]{4,3,2,1,0:T(8,128)S(1)}, f32[4,2,1,6,256]{4,3,2,1,0:T(8,128)S(1)}, u32[]{:S(2)}, u32[]{:S(2)}) collective-permute-start(f32[4,2,1,6,256]{4,3,2,1,0:T(8,128)S(1)} %get-tuple-element.8), channel_id=1, source_target_pairs={{2,0},{4,2},{6,4},{3,1},{5,3},{7,5},{10,8},{12,10},{14,12},{11,9},... | collective-permute-start | bytes 147464 | tf_op jit(solution)/shard_map/ppermute | solution.py:558
  12.3 5.1 %multipole.1 = bf16[32,4,640]{2,1,0:T(4,128)(2,1)} custom-call(s32[2,4,4]{2,1,0:T(4,128)} %counts.1, s32[4]{0:T(128)} %owned.1, f32[3,2,4,4,256]{4,3,2,1,0:T(4,128)} %offsets.3, f32[2,4,4,256]{3,2,1,0:T(4,128)} %charges.1, f32[121,8,121]{2,1,0:T(8,128)} %bitcast.6, s32[4,189]{1,0:T(4,128)} %sources.1, s32[4,189]{1,0:T(4,128)} %classes.1), custom_call_target="tpu_custom_call" | custom-call | tf_op jit(solution)/shard_map/multipole/pallas_call | solution.py:401
  17.4 6.0 %all-to-all-start = ((bf16[32,4,640]{2,1,0:T(4,128)(2,1)}), bf16[32,4,640]{2,1,0:T(4,128)(2,1)S(1)}, u32[]{:S(2)}, u32[]{:S(2)}) async-start(bf16[32,4,640]{2,1,0:T(4,128)(2,1)} %multipole.1), calls=%async_computation | async-start | bytes 327680 | tf_op jit(solution)/shard_map/all_to_all | solution.py:580
  23.4 0.0 collective-permute-done.1
  23.4 0.0 collective-permute-done.2
  23.4 1.0 %pad_maximum_fusion.middle = f32[4,2,6,6,256]{4,3,2,1,0:T(8,128)S(1)} fusion(f32[4,2,1,6,256]{4,3,2,1,0:T(8,128)S(1)} %collective-permute-done.2, f32[4,2,4,1,256]{4,3,2,1,0:T(1,128)S(1)} %get-tuple-element.10, f32[1,2,4,4,256]{4,3,2,1,0:T(4,128)S(1)} %select_bitcast_fusion, f32[3,2,4,4,256]{4,3,2,1,0:T(4,128)} %offsets.3, ...), kind=kLoop, calls=%fused_computation | loop fusion | flops 368640 | bytes 589824 | tf_op jit(solution)/shard_map/concatenate | solution.py:572
  24.5 3.4 %collective-permute-start.3 = (f32[4,1,6,6,256]{4,3,2,1,0:T(8,128)S(1)}, f32[4,1,6,6,256]{4,3,2,1,0:T(8,128)S(1)}, u32[]{:S(2)}, u32[]{:S(2)}) collective-permute-start(f32[4,1,6,6,256]{4,3,2,1,0:T(8,128)S(1)} %get-tuple-element.6), channel_id=1, source_target_pairs={{0,8},{8,16},{16,24},{1,9},{9,17},{17,25},{2,10},{10,18},{18,26},{... | collective-permute-start | bytes 442376 | tf_op jit(solution)/shard_map/ppermute | solution.py:557
  27.9 2.6 %collective-permute-start.4 = (f32[4,1,6,6,256]{4,3,2,1,0:T(8,128)S(1)}, f32[4,1,6,6,256]{4,3,2,1,0:T(8,128)S(1)}, u32[]{:S(2)}, u32[]{:S(2)}) collective-permute-start(f32[4,1,6,6,256]{4,3,2,1,0:T(8,128)S(1)} %get-tuple-element.5), channel_id=1, source_target_pairs={{8,0},{16,8},{24,16},{9,1},{17,9},{25,17},{10,2},{18,10},{26,18},{... | collective-permute-start | bytes 442376 | tf_op jit(solution)/shard_map/ppermute | solution.py:558
  30.5 0.7 broadcast_minimum_fusion.counts
  31.2 0.0 copy-start
  31.2 0.0 copy-start.1
  31.2 2.1 %collective-permute-done.3.lower = f32[4,1,6,6,256]{4,3,2,1,0:T(8,128)S(1)} collective-permute-done((f32[4,1,6,6,256]{4,3,2,1,0:T(8,128)S(1)}, f32[4,1,6,6,256]{4,3,2,1,0:T(8,128)S(1)}, u32[]{:S(2)}, u32[]{:S(2)}) %collective-permute-start.3) | collective-permute-done | bytes 147488 | tf_op jit(solution)/shard_map/ppermute | solution.py:557
  33.3 3.1 %collective-permute-done.4.upper = f32[4,1,6,6,256]{4,3,2,1,0:T(8,128)S(1)} collective-permute-done((f32[4,1,6,6,256]{4,3,2,1,0:T(8,128)S(1)}, f32[4,1,6,6,256]{4,3,2,1,0:T(8,128)S(1)}, u32[]{:S(2)}, u32[]{:S(2)}) %collective-permute-start.4) | collective-permute-done | bytes 147488 | tf_op jit(solution)/shard_map/ppermute | solution.py:558
  36.4 29.0 %near.1 = f32[32,256]{1,0:T(8,128)S(1)} custom-call(s32[2,4,4]{2,1,0:T(4,128)S(1)} %broadcast_minimum_fusion.counts, f32[4,1,6,6,256]{4,3,2,1,0:T(8,128)S(1)} %collective-permute-done.3.lower, f32[4,2,6,6,256]{4,3,2,1,0:T(8,128)S(1)} %pad_maximum_fusion.middle, f32[4,1,6,6,256]{4,3,2,1,0:T(8,128)S(1)} %collective-permute-done.4.upper), custom_call_target="tpu_custom_call" | custom-call | flops 9059696640 | bytes 589824 | tf_op jit(solution)/shard_map/near/pallas_call | solution.py:185
  65.4 0.0 all-to-all-done.arrived
  65.4 0.0 copy-done
  65.5 0.0 copy-done.1
  65.5 8.0 %translate.1 = f32[2,4,4,256]{3,2,1,0:T(4,128)} custom-call(s32[1]{0:T(128)} %bitcast.mine, s32[2,4,4]{2,1,0:T(4,128)S(1)} %broadcast_minimum_fusion.counts, bf16[32,4,640]{2,1,0:T(4,128)(2,1)S(1)} %all-to-all-done.arrived, bf16[121,121,256]{2,1,0:T(8,128)(2,1)} %remote.1, f32[3,2,4,4,256]{4,3,2,1,0:T(4,128)S(1)} %copy-done, f32[32,256]{1,0:T(8,128)S(1)} %near.1, ...), custom_call_target="tpu_custom_call" | custom-call | tf_op jit(solution)/shard_map/translate/pallas_call | solution.py:523
  (2 shorter events, 0.1 us)
Async XLA Ops:
  1.9 4.0 %collective-permute-start = (f32[4,2,4,1,256]{4,3,2,1,0:T(1,128)S(1)}, f32[4,2,4,1,256]{4,3,2,1,0:T(1,128)S(1)}, u32[]{:S(2)}, u32[]{:S(2)}) collective-permute-start(f32[4,2,4,1,256]{4,3,2,1,0:T(1,128)S(1)} %broadcast_select_fusion.2), channel_id=1, source_target_pairs={{0,1},{1,0},{2,3},{3,2},{4,5},{5,4},{6,7},{7,6},{8,9},{9,8},{10,11... | collective-permute-start | bytes 98312 | tf_op jit(solution)/shard_map/ppermute | solution.py:552
  6.7 16.7 %collective-permute-start.1 = (f32[4,2,1,6,256]{4,3,2,1,0:T(8,128)S(1)}, f32[4,2,1,6,256]{4,3,2,1,0:T(8,128)S(1)}, u32[]{:S(2)}, u32[]{:S(2)}) collective-permute-start(f32[4,2,1,6,256]{4,3,2,1,0:T(8,128)S(1)} %get-tuple-element.7), channel_id=1, source_target_pairs={{0,2},{2,4},{4,6},{1,3},{3,5},{5,7},{8,10},{10,12},{12,14},{9,11},... | collective-permute-start | bytes 147464 | tf_op jit(solution)/shard_map/ppermute | solution.py:557
  8.6 14.8 %collective-permute-start.2 = (f32[4,2,1,6,256]{4,3,2,1,0:T(8,128)S(1)}, f32[4,2,1,6,256]{4,3,2,1,0:T(8,128)S(1)}, u32[]{:S(2)}, u32[]{:S(2)}) collective-permute-start(f32[4,2,1,6,256]{4,3,2,1,0:T(8,128)S(1)} %get-tuple-element.8), channel_id=1, source_target_pairs={{2,0},{4,2},{6,4},{3,1},{5,3},{7,5},{10,8},{12,10},{14,12},{11,9},... | collective-permute-start | bytes 147464 | tf_op jit(solution)/shard_map/ppermute | solution.py:558
  17.4 48.0 %all-to-all-start = ((bf16[32,4,640]{2,1,0:T(4,128)(2,1)}), bf16[32,4,640]{2,1,0:T(4,128)(2,1)S(1)}, u32[]{:S(2)}, u32[]{:S(2)}) async-start(bf16[32,4,640]{2,1,0:T(4,128)(2,1)} %multipole.1), calls=%async_computation | async-start | bytes 327680 | tf_op jit(solution)/shard_map/all_to_all | solution.py:580
  24.5 8.8 %collective-permute-start.3 = (f32[4,1,6,6,256]{4,3,2,1,0:T(8,128)S(1)}, f32[4,1,6,6,256]{4,3,2,1,0:T(8,128)S(1)}, u32[]{:S(2)}, u32[]{:S(2)}) collective-permute-start(f32[4,1,6,6,256]{4,3,2,1,0:T(8,128)S(1)} %get-tuple-element.6), channel_id=1, source_target_pairs={{0,8},{8,16},{16,24},{1,9},{9,17},{17,25},{2,10},{10,18},{18,26},{... | collective-permute-start | bytes 442376 | tf_op jit(solution)/shard_map/ppermute | solution.py:557
  27.9 8.5 %collective-permute-start.4 = (f32[4,1,6,6,256]{4,3,2,1,0:T(8,128)S(1)}, f32[4,1,6,6,256]{4,3,2,1,0:T(8,128)S(1)}, u32[]{:S(2)}, u32[]{:S(2)}) collective-permute-start(f32[4,1,6,6,256]{4,3,2,1,0:T(8,128)S(1)} %get-tuple-element.5), channel_id=1, source_target_pairs={{8,0},{16,8},{24,16},{9,1},{17,9},{25,17},{10,2},{18,10},{26,18},{... | collective-permute-start | bytes 442376 | tf_op jit(solution)/shard_map/ppermute | solution.py:558
  31.2 34.3 %copy-start = (f32[3,2,4,4,256]{4,3,2,1,0:T(4,128)S(1)}, f32[3,2,4,4,256]{4,3,2,1,0:T(4,128)}, u32[]{:S(2)}) copy-start(f32[3,2,4,4,256]{4,3,2,1,0:T(4,128)} %offsets.3) | copy-start | bytes 294916
  31.2 34.3 %copy-start.1 = (f32[8,121,121]{2,0,1:T(8,128)S(1)}, f32[8,121,121]{2,0,1:T(8,128)}, u32[]{:S(2)}) copy-start(f32[8,121,121]{2,0,1:T(8,128)} %param.17) | copy-start | bytes 1405540

commit v5 on v3

--- a/solution.py
+++ b/solution.py
@@ -158,7 +158,7 @@
 
     fill_left(0)
     total[...] = jnp.zeros_like(total)
-    step = 32
+    step = 16
 
     def choose(leaf, pieces, low, high):
         if high - low == 1:
@@ -412,7 +412,7 @@
     )(counts, owned, offsets, charges, upward, sources, classes)
 
 
-FETCHES = 11
+FETCHES = 4
 
 
 def translate_body(info, mine, counts, arrived, remote, offsets, near, downward, out, *scratch):
@@ -484,12 +484,12 @@
         sums[start : start + chunk, :] = total
     gather = mask(iota((128, 128), 0) // span == iota((128, 128), 1))
     local = sum(multiply(piece, gather) for piece in split3(sums[...]))
-    parts = split3(local)
-    result = jnp.zeros((coef * 8, 128), jnp.float32)
-    for j, left in enumerate(split3(downward[...].reshape(coef * 8, coef))):
-        for right in parts[0 : 3 - j]:
-            result = result + multiply(left, right)
-    spread_local[...] = result
+    first, second, _ = split3(local)
+    for start in range(0, coef, chunk):
+        rows = downward[start : start + chunk].reshape(chunk * 8, coef)
+        upper, lower, _ = split3(rows)
+        result = multiply(upper, first) + (multiply(upper, second) + multiply(lower, first))
+        spread_local[8 * start : 8 * (start + chunk), :] = result
     for parent in range(per_device):
         rows = slice(8 * parent, 8 * parent + 8)
         total = jnp.zeros((8, width), jnp.float32)
@@ -529,6 +529,7 @@
             pltpu.VMEM((8 * coef, 128), jnp.float32),
             pltpu.SemaphoreType.DMA((coef,)),
         ],
+        compiler_params=pltpu.CompilerParams(vmem_limit_bytes=50 << 20),
         name="translate",
     )(mine, counts, table, matrix, offsets, near, downward)
 
@@ -557,6 +558,7 @@
     per_device = cells[0] * cells[1] * cells[2] // 8
     peers = tuple(lax.axis_size(axis) for axis in MESH_AXES)
     total_parents = per_device * peers[0] * peers[1] * peers[2]
+    sizes = jnp.minimum(counts, charges.shape[3])
     slot_ids = jnp.arange(charges.shape[3], dtype=jnp.int32)
     charge_live = jnp.where(slot_ids[None, None, None, :] < counts[..., None], charges, 0.0)
     padded = jnp.concatenate([offsets, charge_live[None]], 0)
@@ -571,11 +573,11 @@
     )
     table = lax.all_to_all(spread, MESH_AXES, 0, 0)
 
-    near = near_field(counts, slabs, cells)
+    near = near_field(sizes, slabs, cells)
     mine = (lax.axis_index(MESH_AXES) * per_device).astype(jnp.int32).reshape(1)
     downward = l2l.transpose(1, 0, 2)
     lists = list_sources.shape[1]
-    return translate(mine, counts, table, m2l, offsets, near, downward, lists, wide)
+    return translate(mine, sizes, table, m2l, offsets, near, downward, lists, wide)
 
 
 def solution(mesh):

time: 75.3 us -> 74 us (0.983)
  the two profiles are of different devices: /device:TPU:31 before, /device:TPU:14 now
where the time goes in v5:
time: 74 us; the launch traced here: 73.5 us
  Pallas kernels  42 us (57%)
  starting transfers between devices  18.1 us (24%)
  waiting for transfers between devices  8.65 us (12%)
  other arithmetic  4.4 us (6%)
    pallas_call x1, Pallas kernels, near_field(): pl.pallas_call(functools.partial(near_body, cells), out_shape=jax.ShapeDt...  28.6 us
    pallas_call x1, Pallas kernels, translate(): pl.pallas_call(functools.partial(translate_body, (cells, per_device, list...  8.32 us
    ppermute x2, starting transfers between devices, padded_along(): after = lax.ppermute(leading, axis, [(j, i) for i, j in up])  6.27 us
    all_to_all x1, starting transfers between devices, per_block(): table = lax.all_to_all(spread, MESH_AXES, 0, 0)  5.96 us
    ppermute x2, starting transfers between devices, padded_along(): before = lax.ppermute(last, axis, up)  5.32 us
    pallas_call x1, Pallas kernels, multipole(): pl.pallas_call(functools.partial(multipole_body, (cells, peers, wide)), o...  5.13 us
    ppermute x1, waiting for transfers between devices, padded_along(): lax.ppermute(jnp.where(upper, leading, last), axis, [(0, 1), (1, 0)])  3.41 us
    ppermute x2, waiting for transfers between devices, padded_along(): after = lax.ppermute(leading, axis, [(j, i) for i, j in up])  3.14 us
  transfers between devices with their start and end apart: 6, of which 3 were waited for; matrix products, arithmetic and copies ran while one was open for 2% of the time, Pallas kernels for 46%

profile of v5, /device:TPU:14, one launch (start us, length us, event | category | flops | bytes accessed | tf_op | source)
XLA Modules:
  0.0 73.5 jit_solution(4719248841224008651)
XLA Ops:
  0.0 0.8 %select_bitcast_fusion = f32[1,2,4,4,256]{4,3,2,1,0:T(4,128)S(1)} fusion(f32[2,4,4,256]{3,2,1,0:T(4,128)} %charges.1, s32[2,4,4]{2,1,0:T(4,128)} %counts.1), kind=kLoop, calls=%fused_computation.9 | loop fusion | flops 16384 | bytes 65664 | tf_op jit(solution)/shard_map/broadcast_in_dim | solution.py:564
  0.8 1.0 %broadcast_select_fusion.2 = f32[4,2,4,1,256]{4,3,2,1,0:T(1,128)S(1)} fusion(pred[]{:T(512)S(6)} %eq.3, f32[1,2,4,4,256]{4,3,2,1,0:T(4,128)S(1)} %select_bitcast_fusion, f32[3,2,4,4,256]{4,3,2,1,0:T(4,128)} %offsets.3), kind=kLoop, calls=%fused_computation.7 | loop fusion | flops 24576 | bytes 163841 | tf_op jit(solution)/shard_map/jit(_where)/select_n | solution.py:546
  1.9 0.6 collective-permute-start
  2.4 3.4 %collective-permute-done = f32[4,2,4,1,256]{4,3,2,1,0:T(1,128)S(1)} collective-permute-done((f32[4,2,4,1,256]{4,3,2,1,0:T(1,128)S(1)}, f32[4,2,4,1,256]{4,3,2,1,0:T(1,128)S(1)}, u32[]{:S(2)}, u32[]{:S(2)}) %collective-permute-start) | collective-permute-done | bytes 32800 | tf_op jit(solution)/shard_map/ppermute | solution.py:546
  5.9 0.8 %pad_maximum_fusion.4 = (f32[4,2,1,6,256]{4,3,2,1,0:T(8,128)S(1)}, f32[4,2,1,6,256]{4,3,2,1,0:T(8,128)S(1)}) fusion(f32[4,2,4,1,256]{4,3,2,1,0:T(1,128)S(1)} %get-tuple-element.10, f32[4,2,4,1,256]{4,3,2,1,0:T(1,128)S(1)} %get-tuple-element.9, f32[1,2,4,4,256]{4,3,2,1,0:T(4,128)S(1)} %select_bitcast_fusion, f32[3,2,4,4,256]{4,3,2,1,0:T(4,128)} %offsets.3), kind=kLoop, calls=%fused_computation.4 | loop fusion | flops 73728 | bytes 294912 | tf_op jit(solution)/shard_map/slice | solution.py:542
  6.7 1.9 %collective-permute-start.1 = (f32[4,2,1,6,256]{4,3,2,1,0:T(8,128)S(1)}, f32[4,2,1,6,256]{4,3,2,1,0:T(8,128)S(1)}, u32[]{:S(2)}, u32[]{:S(2)}) collective-permute-start(f32[4,2,1,6,256]{4,3,2,1,0:T(8,128)S(1)} %get-tuple-element.7), channel_id=1, source_target_pairs={{0,2},{2,4},{4,6},{1,3},{3,5},{5,7},{8,10},{10,12},{12,14},{9,11},... | collective-permute-start | bytes 147464 | tf_op jit(solution)/shard_map/ppermute | solution.py:551
  8.6 3.6 %collective-permute-start.2 = (f32[4,2,1,6,256]{4,3,2,1,0:T(8,128)S(1)}, f32[4,2,1,6,256]{4,3,2,1,0:T(8,128)S(1)}, u32[]{:S(2)}, u32[]{:S(2)}) collective-permute-start(f32[4,2,1,6,256]{4,3,2,1,0:T(8,128)S(1)} %get-tuple-element.8), channel_id=1, source_target_pairs={{2,0},{4,2},{6,4},{3,1},{5,3},{7,5},{10,8},{12,10},{14,12},{11,9},... | collective-permute-start | bytes 147464 | tf_op jit(solution)/shard_map/ppermute | solution.py:552
  12.3 5.1 %multipole.1 = bf16[32,4,640]{2,1,0:T(4,128)(2,1)} custom-call(s32[2,4,4]{2,1,0:T(4,128)} %counts.1, s32[4]{0:T(128)} %owned.1, f32[3,2,4,4,256]{4,3,2,1,0:T(4,128)} %offsets.3, f32[2,4,4,256]{3,2,1,0:T(4,128)} %charges.1, f32[121,8,121]{2,1,0:T(8,128)} %bitcast.6, s32[4,189]{1,0:T(4,128)} %sources.1, s32[4,189]{1,0:T(4,128)} %classes.1), custom_call_target="tpu_custom_call" | custom-call | tf_op jit(solution)/shard_map/multipole/pallas_call | solution.py:400
  17.4 6.0 %all-to-all-start = ((bf16[32,4,640]{2,1,0:T(4,128)(2,1)}), bf16[32,4,640]{2,1,0:T(4,128)(2,1)S(1)}, u32[]{:S(2)}, u32[]{:S(2)}) async-start(bf16[32,4,640]{2,1,0:T(4,128)(2,1)} %multipole.1), calls=%async_computation | async-start | bytes 327680 | tf_op jit(solution)/shard_map/all_to_all | solution.py:574
  23.4 0.0 collective-permute-done.1
  23.4 0.0 collective-permute-done.2
  23.4 1.0 %pad_maximum_fusion.middle = f32[4,2,6,6,256]{4,3,2,1,0:T(8,128)S(1)} fusion(f32[4,2,1,6,256]{4,3,2,1,0:T(8,128)S(1)} %collective-permute-done.2, f32[4,2,4,1,256]{4,3,2,1,0:T(1,128)S(1)} %get-tuple-element.10, f32[1,2,4,4,256]{4,3,2,1,0:T(4,128)S(1)} %select_bitcast_fusion, f32[3,2,4,4,256]{4,3,2,1,0:T(4,128)} %offsets.3, ...), kind=kLoop, calls=%fused_computation | loop fusion | flops 368640 | bytes 589824 | tf_op jit(solution)/shard_map/concatenate | solution.py:566
  24.5 3.4 %collective-permute-start.3 = (f32[4,1,6,6,256]{4,3,2,1,0:T(8,128)S(1)}, f32[4,1,6,6,256]{4,3,2,1,0:T(8,128)S(1)}, u32[]{:S(2)}, u32[]{:S(2)}) collective-permute-start(f32[4,1,6,6,256]{4,3,2,1,0:T(8,128)S(1)} %get-tuple-element.6), channel_id=1, source_target_pairs={{0,8},{8,16},{16,24},{1,9},{9,17},{17,25},{2,10},{10,18},{18,26},{... | collective-permute-start | bytes 442376 | tf_op jit(solution)/shard_map/ppermute | solution.py:551
  27.9 2.6 %collective-permute-start.4 = (f32[4,1,6,6,256]{4,3,2,1,0:T(8,128)S(1)}, f32[4,1,6,6,256]{4,3,2,1,0:T(8,128)S(1)}, u32[]{:S(2)}, u32[]{:S(2)}) collective-permute-start(f32[4,1,6,6,256]{4,3,2,1,0:T(8,128)S(1)} %get-tuple-element.5), channel_id=1, source_target_pairs={{8,0},{16,8},{24,16},{9,1},{17,9},{25,17},{10,2},{18,10},{26,18},{... | collective-permute-start | bytes 442376 | tf_op jit(solution)/shard_map/ppermute | solution.py:552
  30.5 0.7 broadcast_minimum_fusion.counts
  31.2 0.0 copy-start
  31.2 0.0 copy-start.1
  31.2 2.1 %collective-permute-done.3.lower = f32[4,1,6,6,256]{4,3,2,1,0:T(8,128)S(1)} collective-permute-done((f32[4,1,6,6,256]{4,3,2,1,0:T(8,128)S(1)}, f32[4,1,6,6,256]{4,3,2,1,0:T(8,128)S(1)}, u32[]{:S(2)}, u32[]{:S(2)}) %collective-permute-start.3) | collective-permute-done | bytes 147488 | tf_op jit(solution)/shard_map/ppermute | solution.py:551
  33.3 3.1 %collective-permute-done.4.upper = f32[4,1,6,6,256]{4,3,2,1,0:T(8,128)S(1)} collective-permute-done((f32[4,1,6,6,256]{4,3,2,1,0:T(8,128)S(1)}, f32[4,1,6,6,256]{4,3,2,1,0:T(8,128)S(1)}, u32[]{:S(2)}, u32[]{:S(2)}) %collective-permute-start.4) | collective-permute-done | bytes 147488 | tf_op jit(solution)/shard_map/ppermute | solution.py:552
  36.4 28.6 %near.1 = f32[32,256]{1,0:T(8,128)S(1)} custom-call(s32[2,4,4]{2,1,0:T(4,128)S(1)} %broadcast_minimum_fusion.counts, f32[4,1,6,6,256]{4,3,2,1,0:T(8,128)S(1)} %collective-permute-done.3.lower, f32[4,2,6,6,256]{4,3,2,1,0:T(8,128)S(1)} %pad_maximum_fusion.middle, f32[4,1,6,6,256]{4,3,2,1,0:T(8,128)S(1)} %collective-permute-done.4.upper), custom_call_target="tpu_custom_call" | custom-call | flops 9059696640 | bytes 589824 | tf_op jit(solution)/shard_map/near/pallas_call | solution.py:185
  65.0 0.0 all-to-all-done.arrived
  65.0 0.0 copy-done
  65.0 0.0 copy-done.1
  65.0 8.3 %translate.1 = f32[2,4,4,256]{3,2,1,0:T(4,128)} custom-call(s32[1]{0:T(128)} %bitcast.mine, s32[2,4,4]{2,1,0:T(4,128)S(1)} %broadcast_minimum_fusion.counts, bf16[32,4,640]{2,1,0:T(4,128)(2,1)S(1)} %all-to-all-done.arrived, bf16[121,121,256]{2,1,0:T(8,128)(2,1)} %remote.1, f32[3,2,4,4,256]{4,3,2,1,0:T(4,128)S(1)} %copy-done, f32[32,256]{1,0:T(8,128)S(1)} %near.1, ...), custom_call_target="tpu_custom_call" | custom-call | tf_op jit(solution)/shard_map/translate/pallas_call | solution.py:517
  (2 shorter events, 0.1 us)
Async XLA Ops:
  1.9 4.0 %collective-permute-start = (f32[4,2,4,1,256]{4,3,2,1,0:T(1,128)S(1)}, f32[4,2,4,1,256]{4,3,2,1,0:T(1,128)S(1)}, u32[]{:S(2)}, u32[]{:S(2)}) collective-permute-start(f32[4,2,4,1,256]{4,3,2,1,0:T(1,128)S(1)} %broadcast_select_fusion.2), channel_id=1, source_target_pairs={{0,1},{1,0},{2,3},{3,2},{4,5},{5,4},{6,7},{7,6},{8,9},{9,8},{10,11... | collective-permute-start | bytes 98312 | tf_op jit(solution)/shard_map/ppermute | solution.py:546
  6.7 16.7 %collective-permute-start.1 = (f32[4,2,1,6,256]{4,3,2,1,0:T(8,128)S(1)}, f32[4,2,1,6,256]{4,3,2,1,0:T(8,128)S(1)}, u32[]{:S(2)}, u32[]{:S(2)}) collective-permute-start(f32[4,2,1,6,256]{4,3,2,1,0:T(8,128)S(1)} %get-tuple-element.7), channel_id=1, source_target_pairs={{0,2},{2,4},{4,6},{1,3},{3,5},{5,7},{8,10},{10,12},{12,14},{9,11},... | collective-permute-start | bytes 147464 | tf_op jit(solution)/shard_map/ppermute | solution.py:551
  8.6 14.8 %collective-permute-start.2 = (f32[4,2,1,6,256]{4,3,2,1,0:T(8,128)S(1)}, f32[4,2,1,6,256]{4,3,2,1,0:T(8,128)S(1)}, u32[]{:S(2)}, u32[]{:S(2)}) collective-permute-start(f32[4,2,1,6,256]{4,3,2,1,0:T(8,128)S(1)} %get-tuple-element.8), channel_id=1, source_target_pairs={{2,0},{4,2},{6,4},{3,1},{5,3},{7,5},{10,8},{12,10},{14,12},{11,9},... | collective-permute-start | bytes 147464 | tf_op jit(solution)/shard_map/ppermute | solution.py:552
  17.4 47.6 %all-to-all-start = ((bf16[32,4,640]{2,1,0:T(4,128)(2,1)}), bf16[32,4,640]{2,1,0:T(4,128)(2,1)S(1)}, u32[]{:S(2)}, u32[]{:S(2)}) async-start(bf16[32,4,640]{2,1,0:T(4,128)(2,1)} %multipole.1), calls=%async_computation | async-start | bytes 327680 | tf_op jit(solution)/shard_map/all_to_all | solution.py:574
  24.5 8.8 %collective-permute-start.3 = (f32[4,1,6,6,256]{4,3,2,1,0:T(8,128)S(1)}, f32[4,1,6,6,256]{4,3,2,1,0:T(8,128)S(1)}, u32[]{:S(2)}, u32[]{:S(2)}) collective-permute-start(f32[4,1,6,6,256]{4,3,2,1,0:T(8,128)S(1)} %get-tuple-element.6), channel_id=1, source_target_pairs={{0,8},{8,16},{16,24},{1,9},{9,17},{17,25},{2,10},{10,18},{18,26},{... | collective-permute-start | bytes 442376 | tf_op jit(solution)/shard_map/ppermute | solution.py:551
  27.9 8.5 %collective-permute-start.4 = (f32[4,1,6,6,256]{4,3,2,1,0:T(8,128)S(1)}, f32[4,1,6,6,256]{4,3,2,1,0:T(8,128)S(1)}, u32[]{:S(2)}, u32[]{:S(2)}) collective-permute-start(f32[4,1,6,6,256]{4,3,2,1,0:T(8,128)S(1)} %get-tuple-element.5), channel_id=1, source_target_pairs={{8,0},{16,8},{24,16},{9,1},{17,9},{25,17},{10,2},{18,10},{26,18},{... | collective-permute-start | bytes 442376 | tf_op jit(solution)/shard_map/ppermute | solution.py:552
  31.2 33.8 %copy-start = (f32[3,2,4,4,256]{4,3,2,1,0:T(4,128)S(1)}, f32[3,2,4,4,256]{4,3,2,1,0:T(4,128)}, u32[]{:S(2)}) copy-start(f32[3,2,4,4,256]{4,3,2,1,0:T(4,128)} %offsets.3) | copy-start | bytes 294916
  31.2 33.8 %copy-start.1 = (f32[8,121,121]{2,0,1:T(8,128)S(1)}, f32[8,121,121]{2,0,1:T(8,128)}, u32[]{:S(2)}) copy-start(f32[8,121,121]{2,0,1:T(8,128)} %param.17) | copy-start | bytes 1405540
